TPU v7x, 32 devices: a whole 2x2x4 slice. The times are simulated.
32 devices in a mesh: img: 8 (over z, x), head: 4 (over y, core).
Axes of the slice: x: 2, y: 2, z: 4, core: 2. Of those that a mesh axis runs over, the one named last changes fastest.
Arguments:
- media_patches: bfloat16 [32, 5, 256, 1024], P(('img', 'head')), may hold values from -6 to 6
- latent_rows: bfloat16 [32, 5, 64, 1024], P(('img', 'head')), may hold values from -6 to 6
- media_counts: int32 [32], P(('img', 'head')), may hold values from 1 to 5, as said below
- norm_gains: bfloat16 [3, 1024], P(None, ('img', 'head')), may hold values from 0.5 to 1.5
- norm_biases: bfloat16 [3, 1024], P(None, ('img', 'head')), may hold values from -3 to 3
- query_weight: bfloat16 [1024, 512], P(('img', 'head')), may hold values from -0.375 to 0.375
- key_value_weight: bfloat16 [1024, 1024], P(('img', 'head')), may hold values from -0.1875 to 0.1875
- output_weight: bfloat16 [512, 1024], P(('img', 'head')), may hold values from -0.75 to 0.75
- up_weight: bfloat16 [1024, 4096], P('img', 'head'), may hold values from -0.1875 to 0.1875
- down_weight: bfloat16 [4096, 1024], P('head', 'img'), may hold values from -0.125 to 0.125
- cotangent: bfloat16 [32, 5, 64, 1024], P(('img', 'head')), may hold values from -6 to 6
Outputs:
- new_latents: bfloat16 [32, 5, 64, 1024], P(('img', 'head'))
- media_grad: bfloat16 [32, 5, 256, 1024], P(('img', 'head'))
- latent_grad: bfloat16 [32, 5, 64, 1024], P(('img', 'head'))
- gains_grad: float32 [3, 1024], P(None, ('img', 'head'))
- biases_grad: float32 [3, 1024], P(None, ('img', 'head'))
- query_grad: float32 [1024, 512], P(('img', 'head'))
- key_value_grad: float32 [1024, 1024], P(('img', 'head'))
- output_grad: float32 [512, 1024], P(('img', 'head'))
- up_grad: float32 [1024, 4096], P('img', 'head')
- down_grad: float32 [4096, 1024], P('head', 'img')
Inputs may be any that keep to these rules, and one draw needn't show every extreme that they name: `media_counts`: each sample has 5 media slots; the slots whose index is below its count hold images, the others are empty; every draw has a sample with all 5 slots filled and one with a single image.
All inputs are finite; a program needn't handle non-finite values.
Results may differ from a plain program's by a relative error of at most 0.015.
The roundings to bfloat16 on the way count: a program that leaves them out, or rounds other values in their place, can miss the bound.
Values may be sent and summed in bfloat16 or wider, within the bound.
A program may use at most 192 MiB of HBM per device.

v0:
```python
import jax
import jax.numpy as jnp
from jax import lax
from jax.sharding import PartitionSpec as P

HEADS = 8


def layer_norm(values, norm_gain, norm_shift):
    centered = values - jnp.mean(values, axis=-1, keepdims=True)
    variance = jnp.mean(centered * centered, axis=-1, keepdims=True)
    return centered * lax.rsqrt(variance + 1e-05) * norm_gain + norm_shift


def norm_backward(values, norm_gain, norm_shift, upstream):
    primal, pullback = jax.vjp(layer_norm, values, norm_gain, norm_shift)
    return pullback(upstream)


def exact_gelu(values):
    return jax.nn.gelu(values, approximate=False)


def gelu_backward(values, upstream):
    primal, pullback = jax.vjp(exact_gelu, values)
    return pullback(upstream)[0]


def contract_rows(left_side, right_side):
    return lax.dot_general(
        left_side, right_side, (((0,), (0,)), ((), ())), preferred_element_type=jnp.float32
    )


def contract_cols(left_side, right_side):
    return lax.dot_general(
        left_side, right_side, (((1,), (1,)), ((), ())), preferred_element_type=jnp.float32
    )


def per_device(
    media_patches,
    latent_rows,
    media_counts,
    norm_gains,
    norm_biases,
    query_weight,
    key_value_weight,
    output_weight,
    up_weight,
    down_weight,
    cotangent,
):
    samp_local, media_slots, patches, model_width = media_patches.shape
    queries_per = latent_rows.shape[2]
    images = samp_local * media_slots
    keys_per = patches + queries_per
    rows_local = images * queries_per
    gathered = (
        lax.all_gather(query_weight, ("img", "head"), axis=0, tiled=True),
        lax.all_gather(key_value_weight, ("img", "head"), axis=0, tiled=True),
        lax.all_gather(output_weight, ("img", "head"), axis=0, tiled=True),
        lax.all_gather(norm_gains, ("img", "head"), axis=1, tiled=True),
        lax.all_gather(norm_biases, ("img", "head"), axis=1, tiled=True),
    )
    query_full, key_value_full, output_full, gains_low, biases_low = gathered
    norm_gain = gains_low.astype(jnp.float32)
    norm_shift = biases_low.astype(jnp.float32)
    inner_width = query_full.shape[1]
    head_size = inner_width // HEADS
    score_scale = head_size ** (-0.5)
    up_part, down_part = (
        lax.all_gather(up_weight, "img", axis=0, tiled=True),
        lax.all_gather(down_weight, "img", axis=1, tiled=True),
    )
    media_full = media_patches.reshape(images, patches, model_width).astype(jnp.float32)
    latent_full = latent_rows.reshape(images, queries_per, model_width).astype(jnp.float32)
    media_norm = layer_norm(media_full, norm_gain[0], norm_shift[0]).astype(jnp.bfloat16)
    latent_norm = layer_norm(latent_full, norm_gain[1], norm_shift[1]).astype(jnp.bfloat16)
    query_rows = (
        jnp.einsum("ild,de->ile", latent_norm, query_full, preferred_element_type=jnp.float32)
        * score_scale
    ).astype(jnp.bfloat16)
    key_input = jnp.concatenate([media_norm, latent_norm], axis=1)
    key_value_rows = jnp.einsum(
        "ikd,de->ike", key_input, key_value_full, preferred_element_type=jnp.float32
    ).astype(jnp.bfloat16)
    query_heads = (
        query_rows.reshape(images, queries_per, HEADS, head_size)
        .transpose(2, 0, 1, 3)
        .reshape(HEADS, images, queries_per * head_size)
    )
    key_value_heads = (
        key_value_rows.reshape(images, keys_per, 2, HEADS, head_size)
        .transpose(3, 0, 1, 2, 4)
        .reshape(HEADS, images, keys_per, 2 * head_size)
    )
    query_group, key_value_group = (
        lax.all_to_all(query_heads, "head", split_axis=0, concat_axis=1, tiled=True),
        lax.all_to_all(key_value_heads, "head", split_axis=0, concat_axis=1, tiled=True),
    )
    heads_dev = query_group.shape[0]
    group_images = query_group.shape[1]
    query_block = query_group.reshape(heads_dev, group_images, queries_per, head_size)
    key_block = key_value_group[:, :, :, :head_size]
    value_block = key_value_group[:, :, :, head_size:]
    scores = jnp.einsum(
        "hgqe,hgke->hgqk", query_block, key_block, preferred_element_type=jnp.float32
    )
    row_max = jnp.max(scores, axis=-1, keepdims=True)
    weights = jnp.exp(scores - row_max)
    totals = jnp.sum(weights, axis=-1, keepdims=True)
    log_total = row_max + jnp.log(totals)
    probabilities = (weights / totals).astype(jnp.bfloat16)
    attended = jnp.einsum(
        "hgqk,hgke->hgqe", probabilities, value_block, preferred_element_type=jnp.float32
    ).astype(jnp.bfloat16)
    attended_back = lax.all_to_all(
        attended.reshape(heads_dev, group_images, queries_per * head_size),
        "head",
        split_axis=1,
        concat_axis=0,
        tiled=True,
    )
    attended_local = (
        attended_back.reshape(HEADS, images, queries_per, head_size)
        .transpose(1, 2, 0, 3)
        .reshape(images, queries_per, inner_width)
    )
    attn_delta = jnp.einsum(
        "ile,ed->ild", attended_local, output_full, preferred_element_type=jnp.float32
    )
    mid_latent = latent_full + attn_delta
    hidden_in = (
        layer_norm(mid_latent, norm_gain[2], norm_shift[2])
        .astype(jnp.bfloat16)
        .reshape(rows_local, model_width)
    )
    slot_mask = (
        (jnp.arange(media_slots)[None, :] < media_counts[:, None])
        .astype(jnp.float32)
        .reshape(images, 1, 1)
    )
    up_full, down_full = (
        lax.all_gather(up_part, "head", axis=1, tiled=True),
        lax.all_gather(down_part, "head", axis=0, tiled=True),
    )
    pre_act = jnp.dot(hidden_in, up_full, preferred_element_type=jnp.float32)
    act_low = exact_gelu(pre_act).astype(jnp.bfloat16)
    branch_out = jnp.dot(act_low, down_full, preferred_element_type=jnp.float32)
    result = slot_mask * (mid_latent + branch_out.reshape(images, queries_per, model_width))
    new_latents = result.astype(jnp.bfloat16).reshape(latent_rows.shape)
    out_grad = slot_mask * cotangent.reshape(images, queries_per, model_width).astype(jnp.float32)
    branch_grad = out_grad.astype(jnp.bfloat16).reshape(rows_local, model_width)
    act_grad = contract_cols(branch_grad, down_full)
    pre_grad = gelu_backward(pre_act, act_grad).astype(jnp.bfloat16)
    down_grad_whole = contract_rows(act_low, branch_grad)
    up_grad_whole = contract_rows(hidden_in, pre_grad)
    hidden_grad = contract_cols(pre_grad, up_full)
    up_grad_part, down_grad_part = (
        lax.psum_scatter(
            up_grad_whole.astype(jnp.bfloat16), "head", scatter_dimension=1, tiled=True
        ).astype(jnp.float32),
        lax.psum_scatter(
            down_grad_whole.astype(jnp.bfloat16), "head", scatter_dimension=0, tiled=True
        ).astype(jnp.float32),
    )
    up_grad, down_grad = (
        lax.psum_scatter(
            up_grad_part.astype(jnp.bfloat16), "img", scatter_dimension=0, tiled=True
        ).astype(jnp.float32),
        lax.psum_scatter(
            down_grad_part.astype(jnp.bfloat16), "img", scatter_dimension=1, tiled=True
        ).astype(jnp.float32),
    )
    mid_from_norm, gain_ff, bias_ff = norm_backward(
        mid_latent,
        norm_gain[2],
        norm_shift[2],
        hidden_grad.reshape(images, queries_per, model_width),
    )
    mid_grad = out_grad + mid_from_norm
    delta_low = mid_grad.astype(jnp.bfloat16)
    output_weight_grad = jnp.einsum(
        "ile,ild->ed", attended_local, delta_low, preferred_element_type=jnp.float32
    )
    attended_grad = jnp.einsum(
        "ild,ed->ile", delta_low, output_full, preferred_element_type=jnp.float32
    ).astype(jnp.bfloat16)
    grad_heads = (
        attended_grad.reshape(images, queries_per, HEADS, head_size)
        .transpose(2, 0, 1, 3)
        .reshape(HEADS, images, queries_per * head_size)
    )
    grad_group = lax.all_to_all(
        grad_heads, "head", split_axis=0, concat_axis=1, tiled=True
    ).reshape(heads_dev, group_images, queries_per, head_size)
    scores_again = jnp.einsum(
        "hgqe,hgke->hgqk", query_block, key_block, preferred_element_type=jnp.float32
    )
    probs_again = jnp.exp(scores_again - log_total)
    probs_again_low = probs_again.astype(jnp.bfloat16)
    prob_grad = jnp.einsum(
        "hgqe,hgke->hgqk", grad_group, value_block, preferred_element_type=jnp.float32
    )
    value_grad = jnp.einsum(
        "hgqk,hgqe->hgke", probs_again_low, grad_group, preferred_element_type=jnp.float32
    )
    row_dot = jnp.sum(prob_grad * probs_again, axis=-1, keepdims=True)
    score_grad = (probs_again * (prob_grad - row_dot)).astype(jnp.bfloat16)
    query_grad_group = jnp.einsum(
        "hgqk,hgke->hgqe", score_grad, key_block, preferred_element_type=jnp.float32
    ).astype(jnp.bfloat16)
    key_grad = jnp.einsum(
        "hgqk,hgqe->hgke", score_grad, query_block, preferred_element_type=jnp.float32
    )
    key_value_grad_group = jnp.concatenate([key_grad, value_grad], axis=-1).astype(jnp.bfloat16)
    query_back, key_value_back = (
        lax.all_to_all(
            query_grad_group.reshape(heads_dev, group_images, queries_per * head_size),
            "head",
            split_axis=1,
            concat_axis=0,
            tiled=True,
        ),
        lax.all_to_all(key_value_grad_group, "head", split_axis=1, concat_axis=0, tiled=True),
    )
    query_local = (
        query_back.reshape(HEADS, images, queries_per, head_size)
        .transpose(1, 2, 0, 3)
        .reshape(images, queries_per, inner_width)
    )
    key_value_local = (
        key_value_back.reshape(HEADS, images, keys_per, 2, head_size)
        .transpose(1, 2, 3, 0, 4)
        .reshape(images, keys_per, 2 * inner_width)
    )
    query_weight_grad = (
        jnp.einsum("ild,ile->de", latent_norm, query_local, preferred_element_type=jnp.float32)
        * score_scale
    )
    key_value_weight_grad = jnp.einsum(
        "ikd,ike->de", key_input, key_value_local, preferred_element_type=jnp.float32
    )
    key_input_grad = jnp.einsum(
        "ike,de->ikd", key_value_local, key_value_full, preferred_element_type=jnp.float32
    )
    latent_norm_grad = (
        jnp.einsum("ile,de->ild", query_local, query_full, preferred_element_type=jnp.float32)
        * score_scale
        + key_input_grad[:, patches:]
    )
    media_grad_full, gain_media, bias_media = norm_backward(
        media_full, norm_gain[0], norm_shift[0], key_input_grad[:, :patches]
    )
    latent_from_norm, gain_latent, bias_latent = norm_backward(
        latent_full, norm_gain[1], norm_shift[1], latent_norm_grad
    )
    latent_grad_full = mid_grad + latent_from_norm
    gain_terms = jnp.stack([gain_media, gain_latent, gain_ff])
    bias_terms = jnp.stack([bias_media, bias_latent, bias_ff])
    summed = (
        lax.psum_scatter(query_weight_grad, ("img", "head"), scatter_dimension=0, tiled=True),
        lax.psum_scatter(key_value_weight_grad, ("img", "head"), scatter_dimension=0, tiled=True),
        lax.psum_scatter(output_weight_grad, ("img", "head"), scatter_dimension=0, tiled=True),
        lax.psum_scatter(gain_terms, ("img", "head"), scatter_dimension=1, tiled=True),
        lax.psum_scatter(bias_terms, ("img", "head"), scatter_dimension=1, tiled=True),
    )
    media_grad = media_grad_full.astype(jnp.bfloat16).reshape(media_patches.shape)
    latent_grad = latent_grad_full.astype(jnp.bfloat16).reshape(latent_rows.shape)
    return (
        new_latents,
        media_grad,
        latent_grad,
        summed[3],
        summed[4],
        summed[0],
        summed[1],
        summed[2],
        up_grad,
        down_grad,
    )


def solution(mesh):
    return jax.shard_map(
        per_device,
        mesh=mesh,
        in_specs=(
            P(("img", "head"), None, None, None),
            P(("img", "head"), None, None, None),
            P(("img", "head")),
            P(None, ("img", "head")),
            P(None, ("img", "head")),
            P(("img", "head"), None),
            P(("img", "head"), None),
            P(("img", "head"), None),
            P("img", "head"),
            P("head", "img"),
            P(("img", "head"), None, None, None),
        ),
        out_specs=(
            P(("img", "head"), None, None, None),
            P(("img", "head"), None, None, None),
            P(("img", "head"), None, None, None),
            P(None, ("img", "head")),
            P(None, ("img", "head")),
            P(("img", "head"), None),
            P(("img", "head"), None),
            P(("img", "head"), None),
            P("img", "head"),
            P("head", "img"),
        ),
        check_vma=False,
    )
```

profile of v0, /device:TPU:0, one launch (start us, length us, event | category | flops | bytes accessed | tf_op | source)
XLA Modules:
  0.0 1443.3 jit_solution(9617255876339954277)
XLA Ops:
  10.6 51.3 %all-gather.16.cloned.1.call-done = bf16[1024,1024]{1,0:T(8,128)(2,1)} async-done(((bf16[128,1024]{1,0:T(8,128)(2,1)}), bf16[1024,1024]{1,0:T(8,128)(2,1)}) %all-gather.16.cloned.1.call-update) | async-done | bytes 2097168 | tf_op jit(solution)/shard_map/all_gather | solution.py:73
  62.1 50.9 %all-gather.20.cloned.1.call-done = bf16[1024,1024]{1,0:T(8,128)(2,1)} async-done(((bf16[1024,128]{1,0:T(8,128)(2,1)}), bf16[1024,1024]{1,0:T(8,128)(2,1)}) %all-gather.20.cloned.1.call-update) | async-done | bytes 2097168 | tf_op jit(solution)/shard_map/all_gather | solution.py:74
  113.0 38.7 %all-gather = bf16[32,32,3]{1,2,0:T(4,128)(2,1)S(1)} all-gather(bf16[1,32,3]{1,2,0:T(4,128)(2,1)S(1)} %bitcast.285), channel_id=1, replica_groups=mesh['img'=8,'head'=4] {'img','head'}, dimensions={0}, use_global_device_ids=true | all-gather | bytes 6336 | tf_op jit(solution)/shard_map/all_gather | solution.py:63
  151.8 36.7 %all-gather.1 = bf16[32,32,3]{1,2,0:T(4,128)(2,1)S(1)} all-gather(bf16[1,32,3]{1,2,0:T(4,128)(2,1)S(1)} %bitcast.286), channel_id=1, replica_groups=mesh['img'=8,'head'=4] {'img','head'}, dimensions={0}, use_global_device_ids=true | all-gather | bytes 6336 | tf_op jit(solution)/shard_map/all_gather | solution.py:64
  191.9 2.2 fusion.8
  194.1 2.8 fusion.65
  196.9 2.2 reshape.229
  199.0 2.1 copy.173
  201.1 2.4 reshape.230
  203.5 2.0 copy.108
  205.5 4.2 all-to-all-start
  209.6 17.6 %all-gather.12.cloned.1.call-done = bf16[1024,1024]{1,0:T(8,128)(2,1)} async-done(((bf16[32,1024]{1,0:T(8,128)(2,1)}), bf16[1024,1024]{1,0:T(8,128)(2,1)}) %all-gather.12.cloned.1.call-update) | async-done | bytes 2097168 | tf_op jit(solution)/shard_map/all_gather | solution.py:61
  227.2 7.1 convolution_convert_fusion.2
  234.3 5.8 copy.111
  240.2 4.6 copy.112
  244.7 6.0 copy.113
  250.7 5.0 all-to-all-start.1
  258.3 37.5 %all-to-all-done.1 = bf16[8,5,320,128]{3,2,1,0:T(8,128)(2,1)} async-done(((bf16[8,5,320,128]{3,2,1,0:T(8,128)(2,1)}), bf16[8,5,320,128]{3,2,1,0:T(8,128)(2,1)}, u32[]{:S(2)}, u32[]{:S(2)}) %all-to-all-start.1) | async-done | bytes 3276832 | tf_op jit(solution)/shard_map/all_to_all | solution.py:100
  295.8 5.9 copy.114
  301.8 2.5 fusion.94
  309.1 3.5 all-to-all-start.2
  313.7 9.5 all-to-all-done.2
  324.7 1.9 fusion.95
  328.1 17.9 %all-gather.18.cloned.1.call-done = bf16[1024,4096]{1,0:T(8,128)(2,1)} async-done(((bf16[1024,1024]{1,0:T(8,128)(2,1)}), bf16[1024,4096]{1,0:T(8,128)(2,1)}) %all-gather.18.cloned.1.call-update) | async-done | bytes 8388624 | tf_op jit(solution)/shard_map/all_gather | solution.py:145
  345.9 9.0 fusion.97
  354.9 50.8 %all-gather.22.cloned.1.call-done = bf16[4096,1024]{1,0:T(8,128)(2,1)} async-done(((bf16[1024,1024]{1,0:T(8,128)(2,1)}), bf16[4096,1024]{1,0:T(8,128)(2,1)}) %all-gather.22.cloned.1.call-update) | async-done | bytes 8388624 | tf_op jit(solution)/shard_map/all_gather | solution.py:146
  405.7 17.8 %add_convert_fusion.1 = (bf16[320,4096]{1,0:T(8,128)(2,1)}, f32[320,4096]{1,0:T(8,128)S(1)}) fusion(f32[320,4096]{1,0:T(8,128)} %fusion.97, bf16[320,1024]{1,0:T(8,128)(2,1)} %fusion.63, bf16[4096,1024]{1,0:T(8,128)(2,1)} %all-gather.22.cloned.1.call-done), kind=kOutput, calls=%fused_computation.20 | convolution fusion | flops 2778726400 | bytes 22151168 | tf_op jit(solution)/shard_map/dot_general | solution.py:36
  426.2 6.8 convolution_convert_fusion
  433.0 8.6 reduce-scatter.22.cloned.1.call-start
  441.6 9.3 convolution_convert_fusion.1
  450.9 6.3 fusion.96
  457.7 5.2 fusion.98
  469.2 3.5 all-to-all-start.3
  472.7 14.8 %all-to-all-done.3 = bf16[8,5,4096]{2,1,0:T(8,128)(2,1)S(1)} async-done(((bf16[8,5,4096]{2,1,0:T(8,128)(2,1)}), bf16[8,5,4096]{2,1,0:T(8,128)(2,1)S(1)}, u32[]{:S(2)}, u32[]{:S(2)}) %all-to-all-start.3) | async-done | bytes 327712 | tf_op jit(solution)/shard_map/all_to_all | solution.py:195
  488.3 4.2 multiply_reduce_fusion
  494.7 1.7 fusion.48
  496.4 2.4 reshape.266
  498.8 2.1 copy.147
  500.9 4.3 all-to-all-start.5
  505.2 3.2 fusion.28
  509.2 2.5 pad_maximum_fusion
  511.6 5.8 copy.126
  517.5 4.7 all-to-all-start.4
  525.6 57.5 %all-to-all-done.4 = bf16[2,20,320,128]{3,2,0,1:T(8,128)(2,1)} async-done(((bf16[2,20,320,128]{3,2,0,1:T(8,128)(2,1)}), bf16[2,20,320,128]{3,2,0,1:T(8,128)(2,1)}, u32[]{:S(2)}, u32[]{:S(2)}) %all-to-all-start.4) | async-done | bytes 3276832 | tf_op jit(solution)/shard_map/all_to_all | solution.py:226
  583.1 6.0 copy.128
  589.1 2.8 copy.129
  591.9 1.9 copy-done.14
  593.8 4.5 fusion.21
  599.2 2.9 copy-done.3
  604.0 2.8 fusion.9
  609.1 4.0 copy.152
  613.8 3.3 convolution_bitcast_fusion.1
  617.5 3.3 bitcast_multiply_fusion
  620.8 9.7 convolution_bitcast_fusion
  630.6 3.4 fusion.71
  634.0 4.6 fusion.20
  638.5 106.9 %reduce-scatter.28.cloned.1.call-done = f32[32,3]{1,0:T(8,128)} async-done(((f32[1024,3]{1,0:T(8,128)}), f32[32,3]{1,0:T(8,128)}) %reduce-scatter.28.cloned.1.call-update) | async-done | bytes 400
  746.8 133.1 %reduce-scatter.30.cloned.1.call-done = f32[32,3]{1,0:T(8,128)} async-done(((f32[1024,3]{1,0:T(8,128)}), f32[32,3]{1,0:T(8,128)}) %reduce-scatter.30.cloned.1.call-update) | async-done | bytes 400
  881.3 66.2 %reduce-scatter.32.cloned.1.call-done = bf16[128,1024]{1,0:T(8,128)(2,1)} async-done(((bf16[1024,1024]{1,0:T(8,128)(2,1)}), bf16[128,1024]{1,0:T(8,128)(2,1)}) %reduce-scatter.32.cloned.1.call-update) | async-done | bytes 262160
  949.5 69.1 %reduce-scatter.24.cloned.1.call-done = bf16[128,1024]{1,0:T(8,128)(2,1)} async-done(((bf16[1024,1024]{1,0:T(8,128)(2,1)}), bf16[128,1024]{1,0:T(8,128)(2,1)}) %reduce-scatter.24.cloned.1.call-update) | async-done | bytes 262160 | tf_op jit(solution)/shard_map/reduce_scatter | solution.py:169
  1018.5 1.8 convert_element_type.149
  1020.3 138.6 %reduce-scatter.20.cloned.1.call-done = f32[16,1024]{1,0:T(8,128)} async-done(((f32[512,1024]{1,0:T(8,128)}), f32[16,1024]{1,0:T(8,128)}) %reduce-scatter.20.cloned.1.call-update) | async-done | bytes 65552 | tf_op jit(solution)/shard_map/reduce_scatter | solution.py:265
  1158.9 136.5 %reduce-scatter.16.cloned.1.call-done = f32[32,512]{1,0:T(8,128)} async-done(((f32[1024,512]{1,0:T(8,128)}), f32[32,512]{1,0:T(8,128)}) %reduce-scatter.16.cloned.1.call-update) | async-done | bytes 65552 | tf_op jit(solution)/shard_map/reduce_scatter | solution.py:263
  1295.4 140.9 %reduce-scatter.18.cloned.1.call-done = f32[32,1024]{1,0:T(8,128)} async-done(((f32[1024,1024]{1,0:T(8,128)}), f32[32,1024]{1,0:T(8,128)}) %reduce-scatter.18.cloned.1.call-update) | async-done | bytes 131088 | tf_op jit(solution)/shard_map/reduce_scatter | solution.py:264
  (195 shorter events, 44.6 us)
Async XLA Ops:
  7.2 105.8 %copy-start.43 = (bf16[3,32]{1,0:T(4,128)(2,1)S(1)}, bf16[3,32]{1,0:T(4,128)(2,1)}, u32[]{:S(2)}) copy-start(bf16[3,32]{1,0:T(4,128)(2,1)} %param.14) | copy-start | bytes 580
  7.2 144.6 %copy-start.44 = (bf16[3,32]{1,0:T(4,128)(2,1)S(1)}, bf16[3,32]{1,0:T(4,128)(2,1)}, u32[]{:S(2)}) copy-start(bf16[3,32]{1,0:T(4,128)(2,1)} %param.15) | copy-start | bytes 580
  7.2 181.4 %copy-start.5 = (bf16[1,5,64,1024]{3,2,1,0:T(8,128)(2,1)S(1)}, bf16[1,5,64,1024]{3,2,1,0:T(8,128)(2,1)}, u32[]{:S(2)}) copy-start(bf16[1,5,64,1024]{3,2,1,0:T(8,128)(2,1)} %param.12) | copy-start | bytes 1966084
  7.2 182.0 %copy-start.2 = (bf16[1,5,256,1024]{3,2,1,0:T(8,128)(2,1)S(1)}, bf16[1,5,256,1024]{3,2,1,0:T(8,128)(2,1)}, u32[]{:S(2)}) copy-start(bf16[1,5,256,1024]{3,2,1,0:T(8,128)(2,1)} %param.11) | copy-start | bytes 7864324
  7.2 54.8 %all-gather.16.cloned.1.call-start = ((), (), s32[]{:S(2)}) async-start(), calls=%async_computation.18 | async-start | bytes 2359296 | tf_op jit(solution)/shard_map/all_gather | solution.py:73
  8.0 105.0 %all-gather.20.cloned.1.call-start = ((), (), s32[]{:S(2)}) async-start(), calls=%async_computation.20 | async-start | bytes 2359296 | tf_op jit(solution)/shard_map/all_gather | solution.py:74
  8.7 185.4 %all-gather.10.cloned.1.call-start = ((), (), s32[]{:S(2)}) async-start(), calls=%async_computation.15 | async-start | bytes 1081344 | tf_op jit(solution)/shard_map/all_gather | solution.py:60
  9.4 217.8 %all-gather.12.cloned.1.call-start = ((), (), s32[]{:S(2)}) async-start(), calls=%async_computation.16 | async-start | bytes 2162688 | tf_op jit(solution)/shard_map/all_gather | solution.py:61
  10.0 314.7 %all-gather.14.cloned.1.call-start = ((), (), s32[]{:S(2)}) async-start(), calls=%async_computation.17 | async-start | bytes 1081344 | tf_op jit(solution)/shard_map/all_gather | solution.py:62
  10.6 335.3 %all-gather.18.cloned.1.call-start = ((), (), s32[]{:S(2)}) async-start(), calls=%async_computation.19 | async-start | bytes 10485760 | tf_op jit(solution)/shard_map/all_gather | solution.py:145
  62.0 343.7 %all-gather.22.cloned.1.call-start = ((), (), s32[]{:S(2)}) async-start(), calls=%async_computation.21 | async-start | bytes 10485760 | tf_op jit(solution)/shard_map/all_gather | solution.py:146
  188.8 3.0 copy-start.27
  189.2 2.7 copy-start.37
  189.7 2.1 copy-start.25
  190.6 1.3 copy-start.35
  190.6 1.2 copy-start.29
  190.6 1.2 copy-start.31
  190.6 1.2 copy-start.33
  190.7 6.2 copy-start.41
  194.1 33.2 %copy-start.15 = (bf16[5,256,1024]{2,1,0:T(8,128)(2,1)S(1)}, bf16[5,256,1024]{2,1,0:T(8,128)(2,1)}, u32[]{:S(2)}) copy-start(bf16[5,256,1024]{2,1,0:T(8,128)(2,1)} %fusion.8) | copy-start | bytes 7864324
  205.5 45.2 %all-to-all-start = ((bf16[8,5,4096]{2,1,0:T(8,128)(2,1)}), bf16[8,5,4096]{2,1,0:T(8,128)(2,1)}, u32[]{:S(2)}, u32[]{:S(2)}) async-start(bf16[8,5,4096]{2,1,0:T(8,128)(2,1)} %copy.108), calls=%async_computation | async-start | bytes 1048576 | tf_op jit(solution)/shard_map/all_to_all | solution.py:99
  250.7 45.2 %all-to-all-start.1 = ((bf16[8,5,320,128]{3,2,1,0:T(8,128)(2,1)}), bf16[8,5,320,128]{3,2,1,0:T(8,128)(2,1)}, u32[]{:S(2)}, u32[]{:S(2)}) async-start(bf16[8,5,320,128]{3,2,1,0:T(8,128)(2,1)} %copy.113), calls=%async_computation.1 | async-start | bytes 6553600 | tf_op jit(solution)/shard_map/all_to_all | solution.py:100
  258.3 46.0 %copy-start.10 = (bf16[2,20,64,64]{3,2,0,1:T(8,128)(2,1)}, bf16[2,20,64,64]{3,2,0,1:T(8,128)(2,1)S(1)}, u32[]{:S(2)}) copy-start(bf16[2,20,64,64]{3,2,0,1:T(8,128)(2,1)S(1)} %reshape.231) | copy-start | bytes 983044
  301.8 4.5 copy-start.6
  304.3 2.0 copy-start
  306.3 6.3 copy-start.12
  309.1 14.1 all-to-all-start.2
  312.6 296.5 %reduce-scatter.26.cloned.1.call-start = ((), (), s32[]{:S(2)}) async-start(), calls=%async_computation.27 | async-start | bytes 10485760 | tf_op jit(solution)/shard_map/reduce_scatter | solution.py:164
  324.7 30.2 %copy-start.19 = (bf16[5,64,512]{2,1,0:T(8,128)(2,1)}, bf16[5,64,512]{2,1,0:T(8,128)(2,1)S(1)}, u32[]{:S(2)}) copy-start(bf16[5,64,512]{2,1,0:T(8,128)(2,1)S(1)} %reshape.236) | copy-start | bytes 983044
  405.7 17.8 %copy-start.13 = (f32[320,4096]{1,0:T(8,128)S(1)}, f32[320,4096]{1,0:T(8,128)}, u32[]{:S(2)}) copy-start(f32[320,4096]{1,0:T(8,128)} %fusion.97) | copy-start | bytes 15728644
  423.5 2.6 copy-start.22
  424.6 1.6 copy-start.16
  433.0 8.6 copy-start.23
  433.0 180.1 %reduce-scatter.22.cloned.1.call-start = ((), (), s32[]{:S(2)}) async-start(), calls=%async_computation.25 | async-start | bytes 10485760 | tf_op jit(solution)/shard_map/reduce_scatter | solution.py:161
  450.9 6.8 copy-start.17
  462.9 3.7 copy-start.20
  469.2 18.3 %all-to-all-start.3 = ((bf16[8,5,4096]{2,1,0:T(8,128)(2,1)}), bf16[8,5,4096]{2,1,0:T(8,128)(2,1)S(1)}, u32[]{:S(2)}, u32[]{:S(2)}) async-start(bf16[8,5,4096]{2,1,0:T(8,128)(2,1)} %copy.120), calls=%async_computation.3 | async-start | bytes 1048576 | tf_op jit(solution)/shard_map/all_to_all | solution.py:195
  488.3 4.2 copy-start.1
  492.5 2.2 copy-start.7
  500.9 16.6 %all-to-all-start.5 = ((bf16[2,20,4096]{2,0,1:T(2,128)(2,1)}), bf16[2,20,4096]{2,0,1:T(2,128)(2,1)}, u32[]{:S(2)}, u32[]{:S(2)}) async-start(bf16[2,20,4096]{2,0,1:T(2,128)(2,1)} %copy.147), calls=%async_computation.5 | async-start | bytes 655360 | tf_op jit(solution)/shard_map/all_to_all | solution.py:219
  505.2 3.2 copy-start.11
  517.5 65.6 %all-to-all-start.4 = ((bf16[2,20,320,128]{3,2,0,1:T(8,128)(2,1)}), bf16[2,20,320,128]{3,2,0,1:T(8,128)(2,1)}, u32[]{:S(2)}, u32[]{:S(2)}) async-start(bf16[2,20,320,128]{3,2,0,1:T(8,128)(2,1)} %copy.126), calls=%async_computation.4 | async-start | bytes 6553600 | tf_op jit(solution)/shard_map/all_to_all | solution.py:226
  522.2 223.2 %reduce-scatter.28.cloned.1.call-start = ((), (), s32[]{:S(2)}) async-start(), calls=%async_computation.28 | async-start | bytes 540672
  589.1 4.7 copy-start.45
  591.9 1.9 copy-start.14
  593.8 4.5 copy-start.18
  593.8 4.5 copy-start.21
  593.8 4.5 copy-start.28
  593.8 4.5 copy-start.34
  598.3 5.6 copy-start.4
  598.4 3.7 copy-start.3
  598.4 3.7 copy-start.26
  598.4 3.7 copy-start.32
  599.1 4.2 copy-start.9
  602.1 1.2 copy-start.36
  602.1 1.2 copy-start.38
  602.1 1.9 copy-start.30
  607.9 272.1 %reduce-scatter.30.cloned.1.call-start = ((), (), s32[]{:S(2)}) async-start(), calls=%async_computation.29 | async-start | bytes 540672
  609.0 338.5 %reduce-scatter.32.cloned.1.call-start = ((), (), s32[]{:S(2)}) async-start(), calls=%async_computation.30 | async-start | bytes 2359296
  613.0 405.5 %reduce-scatter.24.cloned.1.call-start = ((), (), s32[]{:S(2)}) async-start(), calls=%async_computation.26 | async-start | bytes 2359296 | tf_op jit(solution)/shard_map/reduce_scatter | solution.py:169
  613.1 4.3 copy-start.42
  613.8 545.1 %reduce-scatter.20.cloned.1.call-start = ((), (), s32[]{:S(2)}) async-start(), calls=%async_computation.24 | async-start | bytes 2162688 | tf_op jit(solution)/shard_map/reduce_scatter | solution.py:265
  617.1 678.3 %reduce-scatter.16.cloned.1.call-start = ((), (), s32[]{:S(2)}) async-start(), calls=%async_computation.22 | async-start | bytes 2162688 | tf_op jit(solution)/shard_map/reduce_scatter | solution.py:263
  620.8 815.6 %reduce-scatter.18.cloned.1.call-start = ((), (), s32[]{:S(2)}) async-start(), calls=%async_computation.23 | async-start | bytes 4325376 | tf_op jit(solution)/shard_map/reduce_scatter | solution.py:264
  (4 other events, 3.3 us)
Sparse Core Ops, SparseCore 0:
  10.2 51.7 all-gather.15
  64.0 48.8 all-gather.19
  115.8 51.8 all-gather.9
  170.4 56.7 all-gather.11
  229.9 53.6 all-gather.13
  285.0 60.8 all-gather.17
  347.5 58.2 all-gather.21
  433.1 77.2 reduce-scatter.25
  513.0 93.9 reduce-scatter.21
  609.6 135.8 reduce-scatter.27
  748.3 131.6 reduce-scatter.29
  883.3 64.1 reduce-scatter.31
  951.0 67.4 reduce-scatter.23
  1021.2 137.6 reduce-scatter.19
  1161.6 133.8 reduce-scatter.15
  1298.2 138.1 reduce-scatter.17
where the time goes:
time: 1450 us; the launch traced here: 1440 us
  waiting for transfers between devices  1100 us (76%)
  matrix products  102 us (7%)
  local copies, waits for them, and re-layouts  81.9 us (6%)
  blocking collectives  75.5 us (5%)
  starting transfers between devices  34.5 us (2%)
  other arithmetic  30.6 us (2%)
  between operations  15.9 us (1%)
    unnamed x19, waiting for transfers between devices  310 us
    reduce_scatter x1, waiting for transfers between devices, per_device(): lax.psum_scatter(key_value_weight_grad, ('img', 'head'), scatter_dimensio...  141 us
    reduce_scatter x1, waiting for transfers between devices, per_device(): lax.psum_scatter(output_weight_grad, ('img', 'head'), scatter_dimension=0...  139 us
    reduce_scatter x1, waiting for transfers between devices, per_device(): lax.psum_scatter(query_weight_grad, ('img', 'head'), scatter_dimension=0,...  137 us
    reduce_scatter x1, waiting for transfers between devices, per_device(): lax.psum_scatter(up_grad_part.astype(jnp.bfloat16), 'img', scatter_dimens...  69.1 us
    all_to_all x1, waiting for transfers between devices, per_device(): lax.all_to_all(key_value_grad_group, 'head', split_axis=1, concat_axis=0,...  57.5 us
    all_gather x1, waiting for transfers between devices, per_device(): lax.all_gather(up_weight, 'img', axis=0, tiled=True)  51.3 us
    all_gather x1, waiting for transfers between devices, per_device(): lax.all_gather(down_weight, 'img', axis=1, tiled=True)  50.9 us
  transfers between devices with their start and end apart: 22, of which 16 were waited for; matrix products, arithmetic and copies ran while one was open for 12% of the time, Pallas kernels for 0%

commit v1 on v0

--- a/solution.py
+++ b/solution.py
@@ -1,6 +1,8 @@
 import jax
 import jax.numpy as jnp
 from jax import lax
+from jax.experimental import pallas as pl
+from jax.experimental.pallas import tpu as pltpu
 from jax.sharding import PartitionSpec as P
 
 HEADS = 8
@@ -38,7 +40,7 @@
     )
 
 
-def per_device(
+def gathered_plan(
     media_patches,
     latent_rows,
     media_counts,
@@ -282,9 +284,1049 @@
     )
 
 
+def tpose(values):
+    return jnp.transpose(values, (1, 0))
+
+
+def dot_nn(left_side, right_side):
+    return jnp.dot(left_side, right_side, preferred_element_type=jnp.float32)
+
+
+def block_kernel(
+    counts,
+    media_in,
+    latent_in,
+    cot_in,
+    query_in,
+    key_value_in,
+    output_in,
+    up_in,
+    down_in,
+    norm_in,
+    new_out,
+    media_out,
+    latent_out,
+    norm_out,
+    query_out,
+    key_value_out,
+    output_out,
+    up_out,
+    down_out,
+    slab,
+    query_full,
+    wide,
+    hid,
+    cotr,
+    turned,
+    media_v,
+    media_n,
+    latent_v,
+    latent_n,
+    media_t,
+    latent_t,
+    kv_media,
+    kv_latent,
+    query_v,
+    att_v,
+    att_t,
+    mid_v,
+    pair,
+    grads,
+    xrecv,
+    zrecv,
+    hsend,
+    hrecv,
+    hysend,
+    hyrecv,
+    hown,
+    delta_v,
+    attg_v,
+    qgrad_v,
+    upstream,
+    normg,
+    normv,
+    gacc,
+    gsend,
+    gyr,
+    gzr,
+    gzr_v,
+    loc,
+    at_z,
+    at_x,
+    at_y,
+    at_c,
+    ff_z,
+    ff_x,
+    nb_z,
+    nb_x,
+    nb_y,
+    nb_c,
+    hd_y,
+    hd_c,
+    hd_f,
+    bg_y,
+    bg_c,
+    hp_c,
+    hp_y,
+    rf_x,
+    rf_z,
+    ra_c,
+    ra_y,
+    ra_x,
+    ra_z,
+    gr_c,
+    gr_z,
+    sent,
+    outs,
+):
+    n_z, n_x, n_head = 4, 2, 4
+    img = lax.axis_index("img")
+    head = lax.axis_index("head")
+    z = img // n_x
+    x = img % n_x
+    y = head // 2
+    c = head % 2
+    xp, yp, cp = 1 - x, 1 - y, 1 - c
+    xdev = (z * n_x + xp, head)
+    ydev = (img, yp * 2 + c)
+    cdev = (img, y * 2 + cp)
+    near = (1, 3, 2)
+
+    def zat(k):
+        return (z + k) % n_z
+
+    def zdev(zz):
+        return (zz * n_x + x, head)
+
+    width = media_v.shape[2]
+    slots = latent_v.shape[0]
+    queries = latent_v.shape[1]
+    hidden = up_in.shape[2]
+    inner = query_full.shape[3]
+    f32 = jnp.float32
+    bf16 = jnp.bfloat16
+    scale = (inner // HEADS) ** (-0.5)
+
+    def rcopy(src, dst, sem_s, sem_r, dev):
+        return pltpu.make_async_remote_copy(
+            src_ref=src,
+            dst_ref=dst,
+            send_sem=sem_s,
+            recv_sem=sem_r,
+            device_id=dev,
+            device_id_type=pl.DeviceIdType.MESH,
+        )
+
+    def send(src, dst, sem_s, sem_r, dev):
+        rcopy(src, dst, sem_s, sem_r, dev).start()
+
+    def arrived(ref, sem):
+        pltpu.make_async_copy(ref, ref, sem).wait()
+
+    unit = img * n_head + head
+    local = [
+        pltpu.make_async_copy(key_value_in, slab.at[unit, 0:32], loc.at[0]),
+        pltpu.make_async_copy(output_in, slab.at[unit, 32:48], loc.at[1]),
+        pltpu.make_async_copy(query_in.at[0:16], slab.at[unit, 48:64, 0:inner], loc.at[2]),
+        pltpu.make_async_copy(query_in.at[16:32], slab.at[unit, 48:64, inner:width], loc.at[3]),
+        pltpu.make_async_copy(norm_in, normg.at[head, :, pl.ds(pl.multiple_of(img * 128, 128), 128)], loc.at[4]),
+        pltpu.make_async_copy(up_in, wide.at[pl.ds(img * 4, 4), :, 0:hidden], loc.at[5]),
+        pltpu.make_async_copy(cot_in, pair.at[0:slots], loc.at[6]),
+        pltpu.make_async_copy(latent_in, latent_v, loc.at[7]),
+        pltpu.make_async_copy(media_in, media_v, loc.at[8]),
+    ]
+    for copy in local:
+        copy.start()
+
+    barrier = pltpu.get_barrier_semaphore()
+    peers = [zdev(zat(k)) for k in near] + [xdev, ydev, cdev]
+    for dev in peers:
+        pl.semaphore_signal(barrier, inc=1, device_id=dev, device_id_type=pl.DeviceIdType.MESH)
+    pl.semaphore_wait(barrier, len(peers))
+
+    def lanes(ii):
+        return pl.ds(pl.multiple_of(ii * 128, 128), 128)
+
+    local[4].wait()
+    for k in near:
+        send(norm_in, normg.at[head, :, lanes(img)], sent.at[0], nb_z.at[z], zdev(zat(k)))
+    for copy in local[0:4]:
+        copy.wait()
+
+    def put_slab(uu, sem, dev):
+        send(slab.at[uu], slab.at[uu], sent.at[1], sem, dev)
+
+    for k in near:
+        put_slab(unit, at_z.at[z], zdev(zat(k)))
+    put_slab(unit, at_x.at[z], xdev)
+    put_slab(unit, at_y.at[img], ydev)
+    put_slab(unit, at_c.at[img, y], cdev)
+
+    local[5].wait()
+    down = down_in[...]
+    for j in range(hidden // 128):
+        wide[pl.ds(img * 4, 4), :, hidden + j * 128 : hidden + (j + 1) * 128] = tpose(
+            down[j * 128 : (j + 1) * 128, :]
+        ).reshape(4, 32, 128)
+
+    local[6].wait()
+    filled = counts[0]
+    for m in range(slots):
+        keep = jnp.clip(filled - m, 0, 1).astype(f32)
+        cotr[head * slots + m] = (pair[m].astype(f32) * keep).astype(bf16)
+
+    def nb_wait(kind, idx, ref):
+        arrived(ref, kind.at[idx])
+
+    for k in near:
+        zz = zat(k)
+        arrived(normg.at[head, :, lanes(zz * n_x + x)], nb_z.at[zz])
+    for k in (0,) + near:
+        zz = zat(k)
+        ii = zz * n_x + x
+        send(normg.at[head, :, lanes(ii)], normg.at[head, :, lanes(ii)], sent.at[2], nb_x.at[zz], xdev)
+
+    def at_forward_z(k):
+        zz = zat(k)
+        uu = (zz * n_x + x) * n_head + head
+        arrived(slab.at[uu], at_z.at[zz])
+        put_slab(uu, at_x.at[zz], xdev)
+        put_slab(uu, at_y.at[zz * n_x + x], ydev)
+        put_slab(uu, at_c.at[zz * n_x + x, y], cdev)
+
+    def at_forward_x(k):
+        zz = zat(k)
+        ii = zz * n_x + xp
+        uu = ii * n_head + head
+        arrived(slab.at[uu], at_x.at[zz])
+        put_slab(uu, at_y.at[ii], ydev)
+        put_slab(uu, at_c.at[ii, y], cdev)
+
+    def at_forward_y(ii):
+        uu = ii * n_head + yp * 2 + c
+        arrived(slab.at[uu], at_y.at[ii])
+        put_slab(uu, at_c.at[ii, yp], cdev)
+
+    at_forward_z(1)
+    at_forward_x(0)
+    at_forward_z(3)
+    for k in (0,) + near:
+        zz = zat(k)
+        arrived(normg.at[head, :, lanes(zz * n_x + xp)], nb_x.at[zz])
+    send(normg.at[head], normg.at[head], sent.at[3], nb_y.at[0], ydev)
+    send(normg.at[head], normg.at[head], sent.at[4], nb_c.at[y], cdev)
+    at_forward_z(2)
+
+    def ff_unit(ii, q):
+        return wide.at[ii * 4 + q]
+
+    for q in range(4):
+        for k in near:
+            send(ff_unit(img, q), ff_unit(img, q), sent.at[5], ff_z.at[z, q], zdev(zat(k)))
+    at_forward_x(1)
+    arrived(normg.at[yp * 2 + c], nb_y.at[0])
+    send(normg.at[yp * 2 + c], normg.at[yp * 2 + c], sent.at[4], nb_c.at[yp], cdev)
+    at_forward_x(3)
+    for q in range(4):
+        send(ff_unit(img, q), ff_unit(img, q), sent.at[6], ff_x.at[z, q], xdev)
+    at_forward_x(2)
+    own_cot = cotr.at[pl.ds(head * slots, slots)]
+    send(own_cot, own_cot, sent.at[7], bg_y.at[0], ydev)
+    send(own_cot, own_cot, sent.at[7], bg_c.at[y], cdev)
+
+    arrived(normg.at[y * 2 + cp], nb_c.at[y])
+    arrived(normg.at[yp * 2 + cp], nb_c.at[yp])
+    normv[...] = normg[0] + normg[1] + normg[2] + normg[3]
+
+    def gain(j):
+        return normv[j : j + 1, :]
+
+    def shift(j):
+        return normv[3 + j : 4 + j, :]
+
+    def statistics(values):
+        centered = values - jnp.mean(values, axis=-1, keepdims=True)
+        inverse = lax.rsqrt(jnp.mean(centered * centered, axis=-1, keepdims=True) + 1e-05)
+        return centered * inverse, inverse
+
+    def norm_rows(values, j):
+        return (statistics(values)[0] * gain(j) + shift(j)).astype(bf16)
+
+    half = queries // 2
+
+    def norm_latent(m, carry):
+        for r in range(2):
+            rows = slice(r * half, (r + 1) * half)
+            latent_n[m, rows, :] = norm_rows(latent_v[m, rows, :].astype(f32), 1)
+        return carry
+
+    def norm_media(m, carry):
+        for r in range(2):
+            rows = slice(r * half, (r + 1) * half)
+            media_n[m, rows, :] = norm_rows(media_v[m, rows, :].astype(f32), 0)
+        return carry
+
+    local[7].wait()
+    lax.fori_loop(0, slots, norm_latent, 0)
+    at_forward_y(img)
+    at_forward_y(zat(1) * n_x + x)
+    local[8].wait()
+    blocks = media_v.shape[0]
+    step = blocks // 4
+    order = [z * n_x + xp, zat(3) * n_x + x, zat(2) * n_x + x, zat(1) * n_x + xp, zat(3) * n_x + xp, zat(2) * n_x + xp]
+    for r in range(4):
+        lax.fori_loop(r * step, (r + 1) * step, norm_media, 0)
+        at_forward_y(order[r])
+
+    def turn_media(r, carry):
+        block = media_n[pl.ds(r * 2, 2)].reshape(128, width)
+        for d in range(width // 128):
+            media_t[d * 128 : (d + 1) * 128, pl.ds(pl.multiple_of(r * 128, 128), 128)] = tpose(
+                block[:, d * 128 : (d + 1) * 128]
+            )
+        return carry
+
+    rows_latent = slots * queries
+
+    def turn_latent(source, target, columns):
+        whole = source[...].reshape(rows_latent, columns)
+        for r in range(0, rows_latent, 128):
+            stop = min(r + 128, rows_latent)
+            for d in range(columns // 128):
+                target[d * 128 : (d + 1) * 128, r:stop] = tpose(
+                    whole[r:stop, d * 128 : (d + 1) * 128]
+                )
+
+    turn_latent(latent_n, latent_t, width)
+    at_forward_y(order[4])
+    lax.fori_loop(0, blocks * queries // 128, turn_media, 0)
+    at_forward_y(order[5])
+
+    def ff_forward(e):
+        q = e // 3
+        step_k = e % 3
+        kk = step_k + 1
+        zz = (z + kk) % n_z
+        piece = ff_unit(zz * n_x + x, q)
+        arrived(piece, ff_z.at[zz, q])
+        send(piece, piece, sent.at[6], ff_x.at[zz, q], xdev)
+
+    for e in range(3):
+        ff_forward(e)
+    for ii in range(8):
+        for yy in range(2):
+            arrived(slab.at[ii * n_head + yy * 2 + cp], at_c.at[ii, yy])
+    ff_forward(3)
+
+    query_full[:, 0] = slab[:, 48:64, 0:inner]
+    query_full[:, 1] = slab[:, 48:64, inner:width]
+
+    def query_tile(cols):
+        return query_full[:, :, :, cols].reshape(width, -1)
+
+    def kv_tile(cols):
+        return slab[:, 0:32, cols].reshape(width, -1)
+
+    def out_tile(cols):
+        return slab[:, 32:48, cols].reshape(inner, -1)
+
+    latent_rows_n = latent_n[...].reshape(rows_latent, width)
+
+    def tile(t):
+        return pl.ds(pl.multiple_of(t * 256, 256), 256)
+
+    def query_step(t, carry):
+        query_v[:, :, tile(t)] = (
+            (dot_nn(latent_rows_n, query_full[:, :, :, tile(t)].reshape(width, 256)) * scale)
+            .astype(bf16)
+            .reshape(slots, queries, 256)
+        )
+        return carry
+
+    lax.fori_loop(0, inner // 256, query_step, 0)
+    groups = kv_media.shape[0]
+
+    def kv_step(t, carry):
+        weight = kv_tile(tile(t))
+        kv_latent[:, :, tile(t)] = dot_nn(latent_rows_n, weight).astype(bf16).reshape(slots, queries, 256)
+
+        def over_media(m, carry2):
+            rows = media_n[pl.ds(m * 4, 4)].reshape(256, width)
+            kv_media[m, :, tile(t)] = dot_nn(rows, weight).astype(bf16)
+            return carry2
+
+        return lax.fori_loop(0, groups, over_media, carry)
+
+    lax.fori_loop(0, width // 256, kv_step, 0)
+    ff_forward(4)
+
+    def lane_mask(hh, dtype):
+        lane = lax.broadcasted_iota(jnp.int32, (1, 256), 1)
+        return (lane // queries == hh).astype(f32).astype(dtype)
+
+    def spread(rows):
+        return jnp.concatenate([rows * lane_mask(hh, bf16) for hh in range(4)], axis=0)
+
+    def fold(rows):
+        total = rows[0:queries] * lane_mask(0, f32)
+        for hh in range(1, 4):
+            total = total + rows[hh * queries : (hh + 1) * queries] * lane_mask(hh, f32)
+        return total
+
+    def probabilities(m, g):
+        q_rows = spread(query_v[m, :, tile(g)])
+        k_media = kv_media[m, :, tile(g)]
+        k_latent = kv_latent[m, :, tile(g)]
+        s_media = contract_cols(q_rows, k_media)
+        s_latent = contract_cols(q_rows, k_latent)
+        top = jnp.maximum(
+            jnp.max(s_media, axis=-1, keepdims=True), jnp.max(s_latent, axis=-1, keepdims=True)
+        )
+        e_media = jnp.exp(s_media - top)
+        e_latent = jnp.exp(s_latent - top)
+        total = jnp.sum(e_media, axis=-1, keepdims=True) + jnp.sum(e_latent, axis=-1, keepdims=True)
+        inverse = 1.0 / total
+        return q_rows, k_media, k_latent, e_media * inverse, e_latent * inverse
+
+    def attend(m, g):
+        p_media, p_latent = probabilities(m, g)[3:]
+        v_media = kv_media[m, :, tile(g + 2)]
+        v_latent = kv_latent[m, :, tile(g + 2)]
+        rows = dot_nn(p_media.astype(bf16), v_media) + dot_nn(p_latent.astype(bf16), v_latent)
+        att_v[m, :, tile(g)] = fold(rows).astype(bf16)
+
+    def forward_image(m, carry):
+        attend(m, 0)
+        attend(m, 1)
+        mid_v[m] = latent_v[m].astype(f32) + dot_nn(att_v[m], out_tile(slice(0, width)))
+        for r in range(2):
+            rows = slice(r * half, (r + 1) * half)
+            hid[head * slots + m, rows, :] = norm_rows(mid_v[m, rows, :], 2)
+        piece = hid.at[head * slots + m]
+        send(piece, piece, sent.at[8], hd_y.at[m], ydev)
+        send(piece, piece, sent.at[8], hd_c.at[m], cdev)
+        ff_forward(m + 5)
+        return carry
+
+    lax.fori_loop(0, slots, forward_image, 0)
+
+    other = yp * 2 + c
+    cot_other = cotr.at[pl.ds(other * slots, slots)]
+    arrived(cot_other, bg_y.at[0])
+    send(cot_other, cot_other, sent.at[7], bg_c.at[yp], cdev)
+    turn_latent(att_v, att_t, inner)
+    ff_forward(10)
+    for yy in (y, yp):
+        arrived(cotr.at[pl.ds((yy * 2 + cp) * slots, slots)], bg_c.at[yy])
+
+    all_rows = n_head * slots * queries
+
+    def turn_rows(source, slot):
+        def body(r, carry):
+            block = source[pl.ds(r * 2, 2)].reshape(128, width)
+            for d in range(width // 128):
+                turned[slot, d * 128 : (d + 1) * 128, pl.ds(pl.multiple_of(r * 128, 128), 128)] = tpose(
+                    block[:, d * 128 : (d + 1) * 128]
+                )
+            return carry
+
+        lax.fori_loop(0, all_rows // 128, body, 0)
+
+    turn_rows(cotr, 1)
+    ff_forward(11)
+
+    def hid_forward(m, carry):
+        piece = hid.at[other * slots + m]
+        arrived(piece, hd_y.at[m])
+        send(piece, piece, sent.at[8], hd_f.at[m], cdev)
+        return carry
+
+    lax.fori_loop(0, slots, hid_forward, 0)
+
+    def hid_arrived(m, carry):
+        arrived(hid.at[(y * 2 + cp) * slots + m], hd_c.at[m])
+        arrived(hid.at[(yp * 2 + cp) * slots + m], hd_f.at[m])
+        return carry
+
+    lax.fori_loop(0, slots, hid_arrived, 0)
+    turn_rows(hid, 0)
+
+    def ff_arrived(e, carry):
+        zz = e // 4
+        q = e % 4
+        arrived(ff_unit(zz * n_x + xp, q), ff_x.at[zz, q])
+        return carry
+
+    lax.fori_loop(0, 16, ff_arrived, 0)
+
+    act_at = 4 * slots
+    row_blocks = all_rows // 256
+
+    def wide_tile(start):
+        return wide[:, :, pl.ds(pl.multiple_of(start, 256), 256)].reshape(width, 256)
+
+    def ff_step(t, carry):
+        up = wide_tile(t * 256)
+        dn = wide_tile(hidden + t * 256)
+
+        def over_rows(r, carry2):
+            rows = pl.ds(r * 4, 4)
+            pre = dot_nn(hid[rows].reshape(256, width), up)
+            grad = dot_nn(cotr[rows].reshape(256, width), dn)
+            below = 0.5 * (1.0 + lax.erf(pre * 0.7071067811865476))
+            slope = below + pre * (jnp.exp(-0.5 * pre * pre) * 0.3989422804014327)
+            pair[rows, :, tile(t)] = (grad * slope).astype(bf16).reshape(4, 64, 256)
+            pair[pl.ds(act_at + r * 4, 4), :, tile(t)] = (pre * below).astype(bf16).reshape(4, 64, 256)
+            return carry2
+
+        return lax.fori_loop(0, row_blocks, over_rows, carry)
+
+    lax.fori_loop(0, hidden // 256, ff_step, 0)
+
+    def wide_rows(part, t):
+        return wide[pl.ds(t * 8, 8), :, part * hidden : (part + 1) * hidden].reshape(256, hidden)
+
+    def head_sum(part):
+        def rows_of(hh):
+            return pair[pl.ds(part * act_at + hh * slots, slots)].reshape(rows_latent, hidden)
+
+        for slot, hh in enumerate((yp * 2 + cp, y * 2 + cp)):
+            left = rows_of(hh)
+
+            def to_core(t, carry, left=left, slot=slot):
+                value = contract_cols(left, wide_rows(part, t))
+                hsend[part, slot, :, :, tile(t)] = value.astype(bf16).reshape(slots, queries, 256)
+                return carry
+
+            lax.fori_loop(0, width // 256, to_core, 0)
+            send(hsend.at[part, slot], hrecv.at[part, slot], sent.at[9], hp_c.at[part, slot], cdev)
+        left_y = rows_of(yp * 2 + c)
+        arrived(hrecv.at[part, 0], hp_c.at[part, 0])
+
+        def to_y(t, carry):
+            value = contract_cols(left_y, wide_rows(part, t)).reshape(slots, queries, 256)
+            hysend[part, :, :, tile(t)] = (value + hrecv[part, 0, :, :, tile(t)].astype(f32)).astype(bf16)
+            return carry
+
+        lax.fori_loop(0, width // 256, to_y, 0)
+        send(hysend.at[part], hyrecv.at[part], sent.at[10], hp_y.at[part], ydev)
+        left_own = rows_of(head)
+        arrived(hrecv.at[part, 1], hp_c.at[part, 1])
+
+        def to_own(t, carry):
+            value = contract_cols(left_own, wide_rows(part, t)).reshape(slots, queries, 256)
+            hown[part, :, :, tile(t)] = value + hrecv[part, 1, :, :, tile(t)].astype(f32)
+            return carry
+
+        lax.fori_loop(0, width // 256, to_own, 0)
+
+    arrived(hid.at[0 : 3 * slots], sent.at[8])
+    head_sum(0)
+
+    def grad_unit(u, carry):
+        zz = (z + 1 + u // 2) % n_z
+        part = u % 2
+        left = turned[part, pl.ds(pl.multiple_of(zz * 256, 256), 256), :]
+
+        def over_cols(t, carry2):
+            right = pair[pl.ds(part * act_at, act_at), :, tile(t)].reshape(all_rows, 256)
+            value = dot_nn(left, right).astype(bf16).reshape(2, 128, 256)
+            grads[zz, 0, part, :, tile(t)] = value[0]
+            grads[zz, 1, part, :, tile(t)] = value[1]
+            return carry2
+
+        lax.fori_loop(0, hidden // 256, over_cols, 0)
+        send(grads.at[zz, xp, part], xrecv.at[zz, part], sent.at[11], rf_x.at[zz, part], xdev)
+        return carry
+
+    def sum_unit(u):
+        zz = (z + 1 + u // 2) % n_z
+        part = u % 2
+        arrived(xrecv.at[zz, part], rf_x.at[zz, part])
+
+        def over(r, carry2):
+            rows = pl.ds(pl.multiple_of(r * 16, 16), 16)
+            grads[zz, x, part, rows, :] = (
+                grads[zz, x, part, rows, :].astype(f32) + xrecv[zz, part, rows, :].astype(f32)
+            ).astype(bf16)
+            return carry2
+
+        lax.fori_loop(0, 8, over, 0)
+        send(grads.at[zz, x, part], zrecv.at[z, part], sent.at[12], rf_z.at[z, part], zdev(zz))
+
+    def grad_and_sum(u, carry):
+        grad_unit(u, carry)
+        sum_unit(u - 4)
+        return carry
+
+    lax.fori_loop(0, 4, grad_unit, 0)
+    lax.fori_loop(4, 8, grad_and_sum, 0)
+    head_sum(1)
+    sum_unit(4)
+
+    gacc[...] = jnp.zeros_like(gacc)
+
+    def tally(j, upper, xhat):
+        gacc[j] += jnp.sum((upper * xhat).reshape(-1, 8, width), axis=0)
+        gacc[3 + j] += jnp.sum(upper.reshape(-1, 8, width), axis=0)
+
+    def norm_back(values, j, upper):
+        xhat, inverse = statistics(values)
+        tally(j, upper, xhat)
+        g = upper * gain(j)
+        return inverse * (
+            g - jnp.mean(g, axis=-1, keepdims=True) - xhat * jnp.mean(g * xhat, axis=-1, keepdims=True)
+        )
+
+    arrived(hyrecv.at[0], hp_y.at[0])
+
+    def mid_back(m, carry):
+        for r in range(4):
+            rows = slice(r * 16, (r + 1) * 16)
+            upper = hown[0, m, rows, :] + hyrecv[0, m, rows, :].astype(f32)
+            back = norm_back(mid_v[m, rows, :], 2, upper)
+            total = cotr[head * slots + m, rows, :].astype(f32) + back
+            hown[0, m, rows, :] = total
+            delta_v[m, rows, :] = total.astype(bf16)
+        return carry
+
+    lax.fori_loop(0, slots, mid_back, 0)
+    delta_rows = delta_v[...].reshape(rows_latent, width)
+
+    def att_back(t, carry):
+        weight = slab[pl.ds(t * 16, 16), 32:48, :].reshape(256, width)
+        attg_v[:, :, tile(t)] = contract_cols(delta_rows, weight).astype(bf16).reshape(slots, queries, 256)
+        return carry
+
+    lax.fori_loop(0, inner // 256, att_back, 0)
+
+    gslab = pair
+
+    def gunit(ii, hh_y, hh_c):
+        return ii * 4 + hh_c * 2 + hh_y
+
+    def out_grad_step(t, carry):
+        right = delta_v[:, :, tile(t)].reshape(rows_latent, 256)
+        value = dot_nn(att_t[...], right).astype(bf16)
+        for ii in range(8):
+            for hh in range(4):
+                at = (ii * 4 + hh) * 16
+                gslab[gunit(ii, hh // 2, hh % 2), 32:48, tile(t)] = value[at : at + 16]
+        return carry
+
+    lax.fori_loop(0, width // 256, out_grad_step, 0)
+    sum_unit(5)
+
+    def back_pair(m, g):
+        q_rows, k_media, k_latent, p_media, p_latent = probabilities(m, g)
+        v_media = kv_media[m, :, tile(g + 2)]
+        v_latent = kv_latent[m, :, tile(g + 2)]
+        up_rows = spread(attg_v[m, :, tile(g)])
+        g_media = contract_cols(up_rows, v_media)
+        g_latent = contract_cols(up_rows, v_latent)
+        dotted = jnp.sum(g_media * p_media, axis=-1, keepdims=True) + jnp.sum(
+            g_latent * p_latent, axis=-1, keepdims=True
+        )
+        d_media = (p_media * (g_media - dotted)).astype(bf16)
+        d_latent = (p_latent * (g_latent - dotted)).astype(bf16)
+        qgrad_v[m, :, tile(g)] = fold(dot_nn(d_media, k_media) + dot_nn(d_latent, k_latent)).astype(bf16)
+        kv_media[m, :, tile(g)] = contract_rows(d_media, q_rows).astype(bf16)
+        kv_latent[m, :, tile(g)] = contract_rows(d_latent, q_rows).astype(bf16)
+        kv_media[m, :, tile(g + 2)] = contract_rows(p_media.astype(bf16), up_rows).astype(bf16)
+        kv_latent[m, :, tile(g + 2)] = contract_rows(p_latent.astype(bf16), up_rows).astype(bf16)
+
+    def back_image(m, carry):
+        back_pair(m, 0)
+        back_pair(m, 1)
+        return carry
+
+    lax.fori_loop(0, slots, back_image, 0)
+
+    gcr = hid
+    gyr_v = media_n
+
+    def kv_grad_chunk(zz):
+        rows = pl.ds(pl.multiple_of(zz * 256, 256), 256)
+        left_media = media_t[rows, :]
+        left_latent = latent_t[rows, :]
+
+        def over_kv(t, carry):
+            value = dot_nn(left_media, kv_media[:, :, tile(t)].reshape(groups * 256, 256)) + dot_nn(
+                left_latent, kv_latent[:, :, tile(t)].reshape(rows_latent, 256)
+            )
+            value = value.astype(bf16)
+            for xx in range(2):
+                for hh in range(4):
+                    at = (xx * 4 + hh) * 32
+                    gslab[gunit(zz * n_x + xx, hh // 2, hh % 2), 0:32, tile(t)] = value[at : at + 32]
+            return carry
+
+        lax.fori_loop(0, width // 256, over_kv, 0)
+
+        def over_q(t, carry):
+            value = dot_nn(left_latent, qgrad_v[:, :, tile(t)].reshape(rows_latent, 256)) * scale
+            value = value.astype(bf16)
+            for xx in range(2):
+                for hh in range(4):
+                    at = (xx * 4 + hh) * 32
+                    uu = gunit(zz * n_x + xx, hh // 2, hh % 2)
+                    gslab[uu, 48:64, pl.ds(pl.multiple_of(t * 256, 256), 256)] = value[at : at + 16]
+                    gslab[uu, 48:64, pl.ds(pl.multiple_of(inner + t * 256, 256), 256)] = value[at + 16 : at + 32]
+            return carry
+
+        lax.fori_loop(0, inner // 256, over_q, 0)
+        for xx in range(2):
+            ii = zz * n_x + xx
+            send(
+                gslab.at[pl.ds(ii * 4 + cp * 2, 2)],
+                gcr.at[pl.ds(ii * 2, 2)],
+                sent.at[13],
+                ra_c.at[ii],
+                cdev,
+            )
+
+    def stage_y(zz):
+        for xx in range(2):
+            ii = zz * n_x + xx
+            arrived(gcr.at[pl.ds(ii * 2, 2)], ra_c.at[ii])
+            uu = gunit(ii, yp, c)
+            gslab[uu] = (gslab[uu].astype(f32) + gcr[ii * 2 + yp].astype(f32)).astype(bf16)
+            send(gslab.at[uu], gyr_v.at[ii], sent.at[14], ra_y.at[ii], ydev)
+
+    def upto_y(ii):
+        return (
+            gslab[gunit(ii, y, c)].astype(f32) + gcr[ii * 2 + y].astype(f32) + gyr_v[ii].astype(f32)
+        )
+
+    def stage_x(zz):
+        ii = zz * n_x + xp
+        arrived(gyr_v.at[ii], ra_y.at[ii])
+        uu = gunit(ii, y, c)
+        gslab[uu] = upto_y(ii).astype(bf16)
+        send(gslab.at[uu], gyr_v.at[8 + zz], sent.at[15], ra_x.at[zz], xdev)
+
+    def stage_z(zz, last):
+        ii = zz * n_x + x
+        arrived(gyr_v.at[ii], ra_y.at[ii])
+        arrived(gyr_v.at[8 + zz], ra_x.at[zz])
+        if last:
+            return upto_y(ii) + gyr_v[8 + zz].astype(f32)
+        uu = gunit(ii, y, c)
+        gslab[uu] = (upto_y(ii) + gyr_v[8 + zz].astype(f32)).astype(bf16)
+        send(gslab.at[uu], gzr_v.at[z], sent.at[16], ra_z.at[z], zdev(zz))
+        return None
+
+    chunk = [zat(1), zat(3), zat(2), z]
+    kv_grad_chunk(chunk[0])
+    kv_grad_chunk(chunk[1])
+    stage_y(chunk[0])
+    kv_grad_chunk(chunk[2])
+    stage_y(chunk[1])
+    kv_grad_chunk(chunk[3])
+    stage_y(chunk[2])
+
+    arrived(hyrecv.at[1], hp_y.at[1])
+    new_v = delta_v
+
+    for m in range(slots):
+        keep = jnp.clip(filled - m, 0, 1).astype(f32)
+        for r in range(2):
+            rows = slice(r * half, (r + 1) * half)
+            branch = hown[1, m, rows, :] + hyrecv[1, m, rows, :].astype(f32)
+            new_v[m, rows, :] = ((mid_v[m, rows, :] + branch) * keep).astype(bf16)
+    new_copy = pltpu.make_async_copy(new_v, new_out, outs.at[0])
+    new_copy.start()
+    stage_y(chunk[3])
+
+    def media_back(m, carry):
+        rows = kv_media[m]
+
+        def over(t, carry2):
+            weight = slab[pl.ds(t * 8, 8), 0:32, :].reshape(256, width)
+            upstream[:, tile(t)] = contract_cols(rows, weight)
+            return carry2
+
+        lax.fori_loop(0, width // 256, over, 0)
+
+        def over_rows(r, carry2):
+            at = pl.ds(pl.multiple_of(r * 16, 16), 16)
+            block = m * 4 + r // 4
+            inside = pl.ds(pl.multiple_of((r % 4) * 16, 16), 16)
+            back = norm_back(media_v[block, inside, :].astype(f32), 0, upstream[at, :])
+            media_v[block, inside, :] = back.astype(bf16)
+            return carry2
+
+        lax.fori_loop(0, 16, over_rows, 0)
+        pltpu.make_async_copy(media_v.at[pl.ds(m * 4, 4)], media_out.at[pl.ds(m * 4, 4)], outs.at[1]).start()
+        return carry
+
+    def latent_back_tiles(m, carry):
+        rows = kv_latent[m]
+        query_rows = qgrad_v[m]
+
+        def over(t, carry2):
+            weight = slab[pl.ds(t * 8, 8), 0:32, :].reshape(256, width)
+            query_weight = query_full[pl.ds(t * 8, 8)].reshape(256, inner)
+            upstream[0:queries, tile(t)] = (
+                contract_cols(rows, weight) + contract_cols(query_rows, query_weight) * scale
+            )
+            return carry2
+
+        lax.fori_loop(0, width // 256, over, 0)
+        for r in range(4):
+            at = slice(r * 16, (r + 1) * 16)
+            back = norm_back(latent_v[m, at, :].astype(f32), 1, upstream[at, :])
+            latent_v[m, at, :] = (hown[0, m, at, :] + back).astype(bf16)
+        return carry
+
+    lax.fori_loop(0, slots, latent_back_tiles, 0)
+    latent_copy = pltpu.make_async_copy(latent_v, latent_out, outs.at[2])
+    latent_copy.start()
+    lax.fori_loop(0, 2, media_back, 0)
+    stage_x(chunk[0])
+    stage_x(chunk[1])
+    lax.fori_loop(2, 4, media_back, 0)
+    stage_x(chunk[2])
+    stage_z(chunk[0], False)
+    stage_z(chunk[1], False)
+    lax.fori_loop(4, 5, media_back, 0)
+    stage_x(chunk[3])
+    stage_z(chunk[2], False)
+
+    for j in range(6):
+        gsend[0, j : j + 1, :] = jnp.sum(gacc[j], axis=0, keepdims=True)
+    gsend[0, 6:8, :] = jnp.zeros((2, width), f32)
+    send(gsend.at[0], gyr.at[0], sent.at[17], gr_c.at[0], cdev)
+    arrived(gyr.at[0], gr_c.at[0])
+    gsend[1] = gsend[0] + gyr[0]
+    send(gsend.at[1], gyr.at[1], sent.at[17], gr_c.at[1], ydev)
+    arrived(gyr.at[1], gr_c.at[1])
+    gsend[2] = gsend[1] + gyr[1]
+    send(gsend.at[2], gyr.at[2], sent.at[17], gr_c.at[2], xdev)
+    arrived(gyr.at[2], gr_c.at[2])
+    gsend[3] = gsend[2] + gyr[2]
+    for k in near:
+        zz = zat(k)
+        send(gsend.at[3, :, lanes(zz * n_x + x)], gzr.at[z], sent.at[18], gr_z.at[z], zdev(zz))
+    total = gsend[3, :, lanes(img)]
+    for k in near:
+        zz = zat(k)
+        arrived(gzr.at[zz], gr_z.at[zz])
+        total = total + gzr[zz]
+    norm_out[...] = total
+
+    for part in range(2):
+        arrived(xrecv.at[z, part], rf_x.at[z, part])
+        for k in near:
+            arrived(zrecv.at[zat(k), part], rf_z.at[zat(k), part])
+
+    def up_last(r, carry):
+        rows = pl.ds(pl.multiple_of(r * 16, 16), 16)
+        value = grads[z, x, 0, rows, :].astype(f32) + xrecv[z, 0, rows, :].astype(f32)
+        for k in near:
+            value = value + zrecv[zat(k), 0, rows, :].astype(f32)
+        up_out[rows, :] = value
+        return carry
+
+    lax.fori_loop(0, 8, up_last, 0)
+
+    def down_last(j, carry):
+        cols = pl.ds(pl.multiple_of(j * 128, 128), 128)
+        value = grads[z, x, 1, :, cols].astype(f32) + xrecv[z, 1, :, cols].astype(f32)
+        for k in near:
+            value = value + zrecv[zat(k), 1, :, cols].astype(f32)
+        down_out[cols, :] = tpose(value)
+        return carry
+
+    lax.fori_loop(0, hidden // 128, down_last, 0)
+
+    final = stage_z(chunk[3], True)
+    for k in near:
+        zz = zat(k)
+        arrived(gzr_v.at[zz], ra_z.at[zz])
+        final = final + gzr_v[zz].astype(f32)
+    key_value_out[...] = final[0:32]
+    output_out[...] = final[32:48]
+    query_out[0:16, :] = final[48:64, 0:inner]
+    query_out[16:32, :] = final[48:64, inner:width]
+
+    new_copy.wait()
+    latent_copy.wait()
+    arrived(media_v, outs.at[1])
+    arrived(normg.at[0, :, 0:384], sent.at[0])
+    arrived(slab.at[0:31], sent.at[1])
+    arrived(normg.at[0, :, 0:512], sent.at[2])
+    arrived(normg.at[0], sent.at[3])
+    arrived(normg.at[0:2], sent.at[4])
+    arrived(wide.at[0:12], sent.at[5])
+    arrived(wide.at[0:16], sent.at[6])
+    arrived(cotr.at[0 : 3 * slots], sent.at[7])
+    arrived(hsend, sent.at[9])
+    arrived(hysend, sent.at[10])
+    arrived(xrecv, sent.at[11])
+    arrived(zrecv.at[0:3], sent.at[12])
+    arrived(gcr.at[0:16], sent.at[13])
+    arrived(gyr_v.at[0:8], sent.at[14])
+    arrived(gyr_v.at[0:4], sent.at[15])
+    arrived(gyr_v.at[0:3], sent.at[16])
+    arrived(gyr, sent.at[17])
+    arrived(gzr.at[0:3], sent.at[18])
+
+
+def block_plan(
+    media_patches,
+    latent_rows,
+    media_counts,
+    norm_gains,
+    norm_biases,
+    query_weight,
+    key_value_weight,
+    output_weight,
+    up_weight,
+    down_weight,
+    cotangent,
+):
+    slots, patches, width = media_patches.shape[1:]
+    queries = latent_rows.shape[2]
+    inner = query_weight.shape[1]
+    hidden = up_weight.shape[1]
+    rows_up = up_weight.shape[0]
+    part = norm_gains.shape[1]
+    head = lax.axis_index("head")
+    norm_rows = jnp.concatenate([norm_gains, norm_biases], axis=0).astype(jnp.float32)
+    norm_tile = lax.dynamic_update_slice(
+        jnp.zeros((8, 128), jnp.float32), norm_rows, (0, head * part)
+    )
+    blocks = slots * patches // 64
+    bf16, f32 = jnp.bfloat16, jnp.float32
+    shape = jax.ShapeDtypeStruct
+    hbm = pl.BlockSpec(memory_space=pl.ANY)
+    vmem = pl.BlockSpec(memory_space=pltpu.VMEM)
+    smem = pl.BlockSpec(memory_space=pltpu.SMEM)
+    dma = pltpu.SemaphoreType.DMA
+    all_rows = 4 * slots * queries
+    rows_latent = slots * queries
+    outs = pl.pallas_call(
+        block_kernel,
+        out_shape=(
+            shape((slots, queries, width), bf16),
+            shape((blocks, 64, width), bf16),
+            shape((slots, queries, width), bf16),
+            shape((8, 128), f32),
+            shape(query_weight.shape, f32),
+            shape(key_value_weight.shape, f32),
+            shape(output_weight.shape, f32),
+            shape(up_weight.shape, f32),
+            shape(down_weight.shape, f32),
+        ),
+        in_specs=[smem] + [hbm] * 7 + [vmem, hbm],
+        out_specs=(hbm, hbm, hbm, vmem, vmem, vmem, vmem, vmem, vmem),
+        scratch_shapes=[
+            pltpu.VMEM((32, 64, width), bf16),
+            pltpu.VMEM((32, 2, 16, inner), bf16),
+            pltpu.VMEM((32, 32, 2 * hidden), bf16),
+            pltpu.VMEM((4 * slots, queries, width), bf16),
+            pltpu.VMEM((4 * slots, queries, width), bf16),
+            pltpu.VMEM((2, width, all_rows), bf16),
+            pltpu.VMEM((blocks, 64, width), bf16),
+            pltpu.VMEM((blocks, 64, width), bf16),
+            pltpu.VMEM((slots, queries, width), bf16),
+            pltpu.VMEM((slots, queries, width), bf16),
+            pltpu.VMEM((width, slots * patches), bf16),
+            pltpu.VMEM((width, rows_latent), bf16),
+            pltpu.VMEM((slots, patches, 2 * inner), bf16),
+            pltpu.VMEM((slots, queries, 2 * inner), bf16),
+            pltpu.VMEM((slots, queries, inner), bf16),
+            pltpu.VMEM((slots, queries, inner), bf16),
+            pltpu.VMEM((inner, rows_latent), bf16),
+            pltpu.VMEM((slots, queries, width), f32),
+            pltpu.VMEM((8 * slots, queries, width), bf16),
+            pltpu.VMEM((4, 2, 2, rows_up, hidden), bf16),
+            pltpu.VMEM((4, 2, rows_up, hidden), bf16),
+            pltpu.VMEM((4, 2, rows_up, hidden), bf16),
+            pltpu.VMEM((2, 2, slots, queries, width), bf16),
+            pltpu.VMEM((2, 2, slots, queries, width), bf16),
+            pltpu.VMEM((2, slots, queries, width), bf16),
+            pltpu.VMEM((2, slots, queries, width), bf16),
+            pltpu.VMEM((2, slots, queries, width), f32),
+            pltpu.VMEM((slots, queries, width), bf16),
+            pltpu.VMEM((slots, queries, inner), bf16),
+            pltpu.VMEM((slots, queries, inner), bf16),
+            pltpu.VMEM((patches, width), f32),
+            pltpu.VMEM((4, 8, width), f32),
+            pltpu.VMEM((8, width), f32),
+            pltpu.VMEM((6, 8, width), f32),
+            pltpu.VMEM((4, 8, width), f32),
+            pltpu.VMEM((3, 8, width), f32),
+            pltpu.VMEM((4, 8, 128), f32),
+            pltpu.VMEM((4, 64, width), bf16),
+            dma((9,)),
+            dma((4,)),
+            dma((4,)),
+            dma((8,)),
+            dma((8, 2)),
+            dma((4, 4)),
+            dma((4, 4)),
+            dma((4,)),
+            dma((4,)),
+            dma((1,)),
+            dma((2,)),
+            dma((slots,)),
+            dma((slots,)),
+            dma((slots,)),
+            dma((1,)),
+            dma((2,)),
+            dma((2, 2)),
+            dma((2,)),
+            dma((4, 2)),
+            dma((4, 2)),
+            dma((8,)),
+            dma((8,)),
+            dma((4,)),
+            dma((4,)),
+            dma((3,)),
+            dma((4,)),
+            dma((19,)),
+            dma((3,)),
+        ],
+        compiler_params=pltpu.CompilerParams(
+            collective_id=0, has_side_effects=True, vmem_limit_bytes=67043328
+        ),
+    )(
+        media_counts,
+        media_patches.reshape(blocks, 64, width),
+        latent_rows.reshape(slots, queries, width),
+        cotangent.reshape(slots, queries, width),
+        query_weight,
+        key_value_weight,
+        output_weight,
+        up_weight.reshape(4, rows_up // 4, hidden),
+        down_weight,
+        norm_tile,
+    )
+    new, media_grad, latent_grad, norms, query_grad, key_value_grad, output_grad, up_grad, down_grad = outs
+    norms = lax.dynamic_slice(norms, (0, head * part), (6, part))
+    return (
+        new.reshape(latent_rows.shape),
+        media_grad.reshape(media_patches.shape),
+        latent_grad.reshape(latent_rows.shape),
+        norms[0:3],
+        norms[3:6],
+        query_grad,
+        key_value_grad,
+        output_grad,
+        up_grad,
+        down_grad,
+    )
+
+
+def block_fits(mesh):
+    return mesh.shape["img"] == 8 and mesh.shape["head"] == 4
+
+
 def solution(mesh):
     return jax.shard_map(
-        per_device,
+        block_plan if block_fits(mesh) else gathered_plan,
         mesh=mesh,
         in_specs=(
             P(("img", "head"), None, None, None),

time: 1450 us -> 214 us (0.15)
  waiting for transfers between devices: 1100 us -> 0 us
  Pallas kernels: 0 us -> 199 us
  matrix products: 102 us -> 0 us
  blocking collectives: 75.5 us -> 0 us
  local copies, waits for them, and re-layouts: 81.9 us -> 12.4 us
  starting transfers between devices: 34.5 us -> 0 us
  other arithmetic: 30.6 us -> 0.7 us
  between operations: 15.9 us -> 1.35 us
    reduce_scatter x6 -> x0, waiting for transfers between devices: 485 us -> none  [the longest x1 141 us: per_device(): lax.psum_scatter(key_value_weight_grad, ('img', 'head'), scatter_dimensio...]
    unnamed x19 -> x0, waiting for transfers between devices: 310 us -> none
    pallas_call x0 -> x1, Pallas kernels: none -> 199 us  [block_plan(): pl.pallas_call(block_kernel, out_shape=(shape((slots, queries, width), bf...]
    all_gather x7 -> x0, waiting for transfers between devices: 189 us -> none  [the longest x1 51.3 us: per_device(): lax.all_gather(up_weight, 'img', axis=0, tiled=True)]
    all_to_all x6 -> x0, waiting for transfers between devices: 119 us -> none  [the longest x1 57.5 us: per_device(): lax.all_to_all(key_value_grad_group, 'head', split_axis=1, concat_axis=0,...]
    dot_general x21 -> x0, matrix products: 102 us -> none  [the longest x2 24.1 us: contract_cols(): lax.dot_general(left_side, right_side, (((1,), (1,)), ((), ())), preferre...]
    all_gather x2 -> x0, blocking collectives: 75.5 us -> none  [the longest x1 38.7 us: per_device(): lax.all_gather(norm_gains, ('img', 'head'), axis=1, tiled=True)]
    reshape x19 -> x0, local copies, waits for them, and re-layouts: 25.9 us -> none  [the longest x1 5.96 us: per_device(): key_value_heads = key_value_rows.reshape(images, keys_per, 2, HEADS, head...]
  transfers between devices with their start and end apart: 22 -> 0, of which waited for: 16 -> 0; matrix products, arithmetic and copies ran while one was open for 12% -> 0% of each run, Pallas kernels for 0% -> 0%
where the time goes in v1:
time: 214 us
  Pallas kernels  199 us (93%)
  local copies, waits for them, and re-layouts  12.4 us (6%)
    pallas_call x1, Pallas kernels, block_plan(): pl.pallas_call(block_kernel, out_shape=(shape((slots, queries, width), bf...  199 us
    unnamed x22, local copies, waits for them, and re-layouts  10.7 us

profile of v1, /device:TPU:0, one launch (start us, length us, event | category | flops | bytes accessed | tf_op | source)
XLA Modules:
  0.0 213.7 jit_solution(7518695474076907800)
XLA Ops:
  0.6 0.7 maximum_convert_fusion
  1.4 0.4 dynamic_update_slice.3.norm_in
  1.7 0.0 copy-start.6
  1.8 0.6 copy-done.6
  3.0 199.3 %shard_map.186 = (bf16[5,64,1024]{2,1,0:T(8,128)(2,1)}, bf16[20,64,1024]{2,1,0:T(8,128)(2,1)}, bf16[5,64,1024]{2,1,0:T(8,128)(2,1)}, f32[8,128]{1,0:T(8,128)}, f...) custom-call(s32[1]{0:T(128)S(6)} %copy.30.counts, ...), custom_call_target="tpu_custom_call" | custom-call | tf_op jit(solution)/shard_map/pallas_call | solution.py:1209
  202.3 0.8 constant_dynamic-slice_fusion
  203.0 0.6 fusion
  203.6 2.0 copy.31
  205.6 0.0 copy-start
  205.6 0.0 copy-start.5
  205.6 0.0 copy-start.3
  205.6 0.0 copy-start.4
  205.6 0.0 copy-start.2
  205.6 3.7 %copy.32 = bf16[1,5,256,1024]{3,2,1,0:T(8,128)(2,1)} copy(bf16[1,5,256,1024]{3,2,1,0:T(8,128)(2,1)} %bitcast.7) | data formatting | bytes 5242880
  209.4 0.0 copy-done
  209.4 0.0 copy-start.1
  209.4 0.8 copy.33
  210.2 0.0 copy-done.5
  210.2 0.6 copy.34
  210.8 0.0 copy-done.3
  210.9 0.7 copy.35
  211.5 0.0 copy-done.4
  211.5 0.6 copy.36
  212.1 0.0 copy-done.2
  212.1 0.8 copy.37
  212.9 0.0 copy-done.1
  212.9 0.8 copy.38
  (1 shorter events, 0.0 us)
Async XLA Ops:
  1.7 0.6 copy-start.6
  205.6 3.8 %copy-start = (bf16[5,64,1024]{2,1,0:T(8,128)(2,1)S(1)}, bf16[5,64,1024]{2,1,0:T(8,128)(2,1)}, u32[]{:S(2)}) copy-start(bf16[5,64,1024]{2,1,0:T(8,128)(2,1)} %get-tuple-element.21) | copy-start | bytes 1966084
  205.6 4.6 %copy-start.5 = (f32[32,512]{1,0:T(8,128)S(1)}, f32[32,512]{1,0:T(8,128)}, u32[]{:S(2)}) copy-start(f32[32,512]{1,0:T(8,128)} %get-tuple-element.45) | copy-start | bytes 196612
  205.6 5.2 %copy-start.3 = (f32[32,1024]{1,0:T(8,128)S(1)}, f32[32,1024]{1,0:T(8,128)}, u32[]{:S(2)}) copy-start(f32[32,1024]{1,0:T(8,128)} %get-tuple-element.46) | copy-start | bytes 393220
  205.6 5.9 %copy-start.4 = (f32[16,1024]{1,0:T(8,128)S(1)}, f32[16,1024]{1,0:T(8,128)}, u32[]{:S(2)}) copy-start(f32[16,1024]{1,0:T(8,128)} %get-tuple-element.47) | copy-start | bytes 196612
  205.6 6.5 %copy-start.2 = (f32[128,1024]{1,0:T(8,128)S(1)}, f32[128,1024]{1,0:T(8,128)}, u32[]{:S(2)}) copy-start(f32[128,1024]{1,0:T(8,128)} %get-tuple-element.48) | copy-start | bytes 1572868
  209.4 3.6 %copy-start.1 = (f32[1024,128]{1,0:T(8,128)S(1)}, f32[1024,128]{1,0:T(8,128)}, u32[]{:S(2)}) copy-start(f32[1024,128]{1,0:T(8,128)} %get-tuple-element.49) | copy-start | bytes 1572868

commit v2 on v1

--- a/solution.py
+++ b/solution.py
@@ -6,6 +6,7 @@
 from jax.sharding import PartitionSpec as P
 
 HEADS = 8
+FF_ROWS = 20
 
 
 def layer_norm(values, norm_gain, norm_shift):
@@ -342,7 +343,6 @@
     delta_v,
     attg_v,
     qgrad_v,
-    upstream,
     normg,
     normv,
     gacc,
@@ -635,27 +635,19 @@
     def tile(t):
         return pl.ds(pl.multiple_of(t * 256, 256), 256)
 
-    def query_step(t, carry):
-        query_v[:, :, tile(t)] = (
-            (dot_nn(latent_rows_n, query_full[:, :, :, tile(t)].reshape(width, 256)) * scale)
-            .astype(bf16)
-            .reshape(slots, queries, 256)
-        )
-        return carry
-
-    lax.fori_loop(0, inner // 256, query_step, 0)
+    query_v[...] = (
+        (dot_nn(latent_rows_n, query_full[...].reshape(width, inner)) * scale)
+        .astype(bf16)
+        .reshape(slots, queries, inner)
+    )
     groups = kv_media.shape[0]
+    media_rows_n = media_n[...].reshape(groups * 256, width)
 
     def kv_step(t, carry):
         weight = kv_tile(tile(t))
         kv_latent[:, :, tile(t)] = dot_nn(latent_rows_n, weight).astype(bf16).reshape(slots, queries, 256)
-
-        def over_media(m, carry2):
-            rows = media_n[pl.ds(m * 4, 4)].reshape(256, width)
-            kv_media[m, :, tile(t)] = dot_nn(rows, weight).astype(bf16)
-            return carry2
-
-        return lax.fori_loop(0, groups, over_media, carry)
+        kv_media[:, :, tile(t)] = dot_nn(media_rows_n, weight).astype(bf16).reshape(groups, 256, 256)
+        return carry
 
     lax.fori_loop(0, width // 256, kv_step, 0)
     ff_forward(4)
@@ -760,7 +752,6 @@
     lax.fori_loop(0, 16, ff_arrived, 0)
 
     act_at = 4 * slots
-    row_blocks = all_rows // 256
 
     def wide_tile(start):
         return wide[:, :, pl.ds(pl.multiple_of(start, 256), 256)].reshape(width, 256)
@@ -770,21 +761,26 @@
         dn = wide_tile(hidden + t * 256)
 
         def over_rows(r, carry2):
-            rows = pl.ds(r * 4, 4)
-            pre = dot_nn(hid[rows].reshape(256, width), up)
-            grad = dot_nn(cotr[rows].reshape(256, width), dn)
+            rows = pl.ds(r * FF_ROWS, FF_ROWS)
+            pre = dot_nn(hid[rows].reshape(FF_ROWS * 64, width), up)
+            grad = dot_nn(cotr[rows].reshape(FF_ROWS * 64, width), dn)
             below = 0.5 * (1.0 + lax.erf(pre * 0.7071067811865476))
             slope = below + pre * (jnp.exp(-0.5 * pre * pre) * 0.3989422804014327)
-            pair[rows, :, tile(t)] = (grad * slope).astype(bf16).reshape(4, 64, 256)
-            pair[pl.ds(act_at + r * 4, 4), :, tile(t)] = (pre * below).astype(bf16).reshape(4, 64, 256)
+            pair[rows, :, tile(t)] = (grad * slope).astype(bf16).reshape(FF_ROWS, 64, 256)
+            pair[pl.ds(act_at + r * FF_ROWS, FF_ROWS), :, tile(t)] = (
+                (pre * below).astype(bf16).reshape(FF_ROWS, 64, 256)
+            )
             return carry2
 
-        return lax.fori_loop(0, row_blocks, over_rows, carry)
+        return lax.fori_loop(0, act_at // FF_ROWS, over_rows, carry)
 
     lax.fori_loop(0, hidden // 256, ff_step, 0)
 
     def wide_rows(part, t):
-        return wide[pl.ds(t * 8, 8), :, part * hidden : (part + 1) * hidden].reshape(256, hidden)
+        return wide[pl.ds(t * 16, 16), :, part * hidden : (part + 1) * hidden].reshape(512, hidden)
+
+    def broad(t):
+        return pl.ds(pl.multiple_of(t * 512, 512), 512)
 
     def head_sum(part):
         def rows_of(hh):
@@ -795,30 +791,30 @@
 
             def to_core(t, carry, left=left, slot=slot):
                 value = contract_cols(left, wide_rows(part, t))
-                hsend[part, slot, :, :, tile(t)] = value.astype(bf16).reshape(slots, queries, 256)
+                hsend[part, slot, :, :, broad(t)] = value.astype(bf16).reshape(slots, queries, 512)
                 return carry
 
-            lax.fori_loop(0, width // 256, to_core, 0)
+            lax.fori_loop(0, width // 512, to_core, 0)
             send(hsend.at[part, slot], hrecv.at[part, slot], sent.at[9], hp_c.at[part, slot], cdev)
         left_y = rows_of(yp * 2 + c)
         arrived(hrecv.at[part, 0], hp_c.at[part, 0])
 
         def to_y(t, carry):
-            value = contract_cols(left_y, wide_rows(part, t)).reshape(slots, queries, 256)
-            hysend[part, :, :, tile(t)] = (value + hrecv[part, 0, :, :, tile(t)].astype(f32)).astype(bf16)
+            value = contract_cols(left_y, wide_rows(part, t)).reshape(slots, queries, 512)
+            hysend[part, :, :, broad(t)] = (value + hrecv[part, 0, :, :, broad(t)].astype(f32)).astype(bf16)
             return carry
 
-        lax.fori_loop(0, width // 256, to_y, 0)
+        lax.fori_loop(0, width // 512, to_y, 0)
         send(hysend.at[part], hyrecv.at[part], sent.at[10], hp_y.at[part], ydev)
         left_own = rows_of(head)
         arrived(hrecv.at[part, 1], hp_c.at[part, 1])
 
         def to_own(t, carry):
-            value = contract_cols(left_own, wide_rows(part, t)).reshape(slots, queries, 256)
-            hown[part, :, :, tile(t)] = value + hrecv[part, 1, :, :, tile(t)].astype(f32)
+            value = contract_cols(left_own, wide_rows(part, t)).reshape(slots, queries, 512)
+            hown[part, :, :, broad(t)] = value + hrecv[part, 1, :, :, broad(t)].astype(f32)
             return carry
 
-        lax.fori_loop(0, width // 256, to_own, 0)
+        lax.fori_loop(0, width // 512, to_own, 0)
 
     arrived(hid.at[0 : 3 * slots], sent.at[8])
     head_sum(0)
@@ -828,14 +824,10 @@
         part = u % 2
         left = turned[part, pl.ds(pl.multiple_of(zz * 256, 256), 256), :]
 
-        def over_cols(t, carry2):
-            right = pair[pl.ds(part * act_at, act_at), :, tile(t)].reshape(all_rows, 256)
-            value = dot_nn(left, right).astype(bf16).reshape(2, 128, 256)
-            grads[zz, 0, part, :, tile(t)] = value[0]
-            grads[zz, 1, part, :, tile(t)] = value[1]
-            return carry2
-
-        lax.fori_loop(0, hidden // 256, over_cols, 0)
+        right = pair[pl.ds(part * act_at, act_at)].reshape(all_rows, hidden)
+        value = dot_nn(left, right).astype(bf16).reshape(2, 128, hidden)
+        grads[zz, 0, part] = value[0]
+        grads[zz, 1, part] = value[1]
         send(grads.at[zz, xp, part], xrecv.at[zz, part], sent.at[11], rf_x.at[zz, part], xdev)
         return carry
 
@@ -881,24 +873,19 @@
     arrived(hyrecv.at[0], hp_y.at[0])
 
     def mid_back(m, carry):
-        for r in range(4):
-            rows = slice(r * 16, (r + 1) * 16)
-            upper = hown[0, m, rows, :] + hyrecv[0, m, rows, :].astype(f32)
-            back = norm_back(mid_v[m, rows, :], 2, upper)
-            total = cotr[head * slots + m, rows, :].astype(f32) + back
-            hown[0, m, rows, :] = total
-            delta_v[m, rows, :] = total.astype(bf16)
+        upper = hown[0, m] + hyrecv[0, m].astype(f32)
+        back = norm_back(mid_v[m], 2, upper)
+        total = cotr[head * slots + m].astype(f32) + back
+        hown[0, m] = total
+        delta_v[m] = total.astype(bf16)
         return carry
 
     lax.fori_loop(0, slots, mid_back, 0)
     delta_rows = delta_v[...].reshape(rows_latent, width)
 
-    def att_back(t, carry):
-        weight = slab[pl.ds(t * 16, 16), 32:48, :].reshape(256, width)
-        attg_v[:, :, tile(t)] = contract_cols(delta_rows, weight).astype(bf16).reshape(slots, queries, 256)
-        return carry
-
-    lax.fori_loop(0, inner // 256, att_back, 0)
+    attg_v[...] = (
+        contract_cols(delta_rows, out_tile(slice(0, width))).astype(bf16).reshape(slots, queries, inner)
+    )
 
     gslab = pair
 
@@ -906,15 +893,15 @@
         return ii * 4 + hh_c * 2 + hh_y
 
     def out_grad_step(t, carry):
-        right = delta_v[:, :, tile(t)].reshape(rows_latent, 256)
+        right = delta_v[:, :, broad(t)].reshape(rows_latent, 512)
         value = dot_nn(att_t[...], right).astype(bf16)
         for ii in range(8):
             for hh in range(4):
                 at = (ii * 4 + hh) * 16
-                gslab[gunit(ii, hh // 2, hh % 2), 32:48, tile(t)] = value[at : at + 16]
-        return carry
-
-    lax.fori_loop(0, width // 256, out_grad_step, 0)
+                gslab[gunit(ii, hh // 2, hh % 2), 32:48, broad(t)] = value[at : at + 16]
+        return carry
+
+    lax.fori_loop(0, width // 512, out_grad_step, 0)
     sum_unit(5)
 
     def back_pair(m, g):
@@ -950,31 +937,19 @@
         left_media = media_t[rows, :]
         left_latent = latent_t[rows, :]
 
-        def over_kv(t, carry):
-            value = dot_nn(left_media, kv_media[:, :, tile(t)].reshape(groups * 256, 256)) + dot_nn(
-                left_latent, kv_latent[:, :, tile(t)].reshape(rows_latent, 256)
-            )
-            value = value.astype(bf16)
-            for xx in range(2):
-                for hh in range(4):
-                    at = (xx * 4 + hh) * 32
-                    gslab[gunit(zz * n_x + xx, hh // 2, hh % 2), 0:32, tile(t)] = value[at : at + 32]
-            return carry
-
-        lax.fori_loop(0, width // 256, over_kv, 0)
-
-        def over_q(t, carry):
-            value = dot_nn(left_latent, qgrad_v[:, :, tile(t)].reshape(rows_latent, 256)) * scale
-            value = value.astype(bf16)
-            for xx in range(2):
-                for hh in range(4):
-                    at = (xx * 4 + hh) * 32
-                    uu = gunit(zz * n_x + xx, hh // 2, hh % 2)
-                    gslab[uu, 48:64, pl.ds(pl.multiple_of(t * 256, 256), 256)] = value[at : at + 16]
-                    gslab[uu, 48:64, pl.ds(pl.multiple_of(inner + t * 256, 256), 256)] = value[at + 16 : at + 32]
-            return carry
-
-        lax.fori_loop(0, inner // 256, over_q, 0)
+        value = dot_nn(left_media, kv_media[...].reshape(groups * 256, width)) + dot_nn(
+            left_latent, kv_latent[...].reshape(rows_latent, width)
+        )
+        value = value.astype(bf16)
+        value_q = dot_nn(left_latent, qgrad_v[...].reshape(rows_latent, inner)) * scale
+        value_q = value_q.astype(bf16)
+        for xx in range(2):
+            for hh in range(4):
+                at = (xx * 4 + hh) * 32
+                uu = gunit(zz * n_x + xx, hh // 2, hh % 2)
+                gslab[uu, 0:32, :] = value[at : at + 32]
+                gslab[uu, 48:64, 0:inner] = value_q[at : at + 16]
+                gslab[uu, 48:64, inner:width] = value_q[at + 16 : at + 32]
         for xx in range(2):
             ii = zz * n_x + xx
             send(
@@ -1039,47 +1014,34 @@
     stage_y(chunk[3])
 
     def media_back(m, carry):
-        rows = kv_media[m]
-
-        def over(t, carry2):
-            weight = slab[pl.ds(t * 8, 8), 0:32, :].reshape(256, width)
-            upstream[:, tile(t)] = contract_cols(rows, weight)
+        hown[1, 0:4] = contract_cols(kv_media[m], kv_tile(slice(0, width))).reshape(4, 64, width)
+
+        def over_rows(r, carry2):
+            block = m * 4 + r
+            back = norm_back(media_v[block].astype(f32), 0, hown[1, r])
+            media_v[block] = back.astype(bf16)
             return carry2
 
-        lax.fori_loop(0, width // 256, over, 0)
-
-        def over_rows(r, carry2):
-            at = pl.ds(pl.multiple_of(r * 16, 16), 16)
-            block = m * 4 + r // 4
-            inside = pl.ds(pl.multiple_of((r % 4) * 16, 16), 16)
-            back = norm_back(media_v[block, inside, :].astype(f32), 0, upstream[at, :])
-            media_v[block, inside, :] = back.astype(bf16)
-            return carry2
-
-        lax.fori_loop(0, 16, over_rows, 0)
+        lax.fori_loop(0, 4, over_rows, 0)
         pltpu.make_async_copy(media_v.at[pl.ds(m * 4, 4)], media_out.at[pl.ds(m * 4, 4)], outs.at[1]).start()
         return carry
 
-    def latent_back_tiles(m, carry):
-        rows = kv_latent[m]
-        query_rows = qgrad_v[m]
-
-        def over(t, carry2):
-            weight = slab[pl.ds(t * 8, 8), 0:32, :].reshape(256, width)
-            query_weight = query_full[pl.ds(t * 8, 8)].reshape(256, inner)
-            upstream[0:queries, tile(t)] = (
-                contract_cols(rows, weight) + contract_cols(query_rows, query_weight) * scale
-            )
-            return carry2
-
-        lax.fori_loop(0, width // 256, over, 0)
-        for r in range(4):
-            at = slice(r * 16, (r + 1) * 16)
-            back = norm_back(latent_v[m, at, :].astype(f32), 1, upstream[at, :])
-            latent_v[m, at, :] = (hown[0, m, at, :] + back).astype(bf16)
-        return carry
-
-    lax.fori_loop(0, slots, latent_back_tiles, 0)
+    def latent_back_tiles(t, carry):
+        weight = slab[pl.ds(t * 16, 16), 0:32, :].reshape(512, width)
+        query_weight = query_full[pl.ds(t * 16, 16)].reshape(512, inner)
+        hown[1, :, :, broad(t)] = (
+            contract_cols(kv_latent[...].reshape(rows_latent, width), weight)
+            + contract_cols(qgrad_v[...].reshape(rows_latent, inner), query_weight) * scale
+        ).reshape(slots, queries, 512)
+        return carry
+
+    def latent_back(m, carry):
+        back = norm_back(latent_v[m].astype(f32), 1, hown[1, m])
+        latent_v[m] = (hown[0, m] + back).astype(bf16)
+        return carry
+
+    lax.fori_loop(0, width // 512, latent_back_tiles, 0)
+    lax.fori_loop(0, slots, latent_back, 0)
     latent_copy = pltpu.make_async_copy(latent_v, latent_out, outs.at[2])
     latent_copy.start()
     lax.fori_loop(0, 2, media_back, 0)
@@ -1252,7 +1214,6 @@
             pltpu.VMEM((slots, queries, width), bf16),
             pltpu.VMEM((slots, queries, inner), bf16),
             pltpu.VMEM((slots, queries, inner), bf16),
-            pltpu.VMEM((patches, width), f32),
             pltpu.VMEM((4, 8, width), f32),
             pltpu.VMEM((8, width), f32),
             pltpu.VMEM((6, 8, width), f32),

time: 214 us -> 185 us (0.86)
  Pallas kernels: 199 us -> 170 us
    pallas_call x1, Pallas kernels: 199 us -> 170 us  [block_plan(): pl.pallas_call(block_kernel, out_shape=(shape((slots, queries, width), bf...]
where the time goes in v2:
time: 185 us
  Pallas kernels  170 us (92%)
  local copies, waits for them, and re-layouts  12.4 us (7%)
    pallas_call x1, Pallas kernels, block_plan(): pl.pallas_call(block_kernel, out_shape=(shape((slots, queries, width), bf...  170 us
    unnamed x22, local copies, waits for them, and re-layouts  10.7 us

profile of v2, /device:TPU:0, one launch (start us, length us, event | category | flops | bytes accessed | tf_op | source)
XLA Modules:
  0.0 184.7 jit_solution(7485094970809513884)
XLA Ops:
  0.6 0.7 maximum_convert_fusion
  1.4 0.4 dynamic_update_slice.3.norm_in
  1.7 0.0 copy-start.6
  1.8 0.6 copy-done.6
  3.0 170.2 %shard_map.186 = (bf16[5,64,1024]{2,1,0:T(8,128)(2,1)}, bf16[20,64,1024]{2,1,0:T(8,128)(2,1)}, bf16[5,64,1024]{2,1,0:T(8,128)(2,1)}, f32[8,128]{1,0:T(8,128)}, f...) custom-call(s32[1]{0:T(128)S(6)} %copy.30.counts, ...), custom_call_target="tpu_custom_call" | custom-call | tf_op jit(solution)/shard_map/pallas_call | solution.py:1171
  173.2 0.8 constant_dynamic-slice_fusion
  174.0 0.6 fusion
  174.6 2.0 %copy.31 = bf16[1,5,64,1024]{3,2,1,0:T(8,128)(2,1)} copy(bf16[1,5,64,1024]{3,2,1,0:T(8,128)(2,1)} %bitcast.10) | data formatting | bytes 1310720
  176.6 0.0 copy-start
  176.6 0.0 copy-start.5
  176.6 0.0 copy-start.3
  176.6 0.0 copy-start.4
  176.6 0.0 copy-start.2
  176.6 3.7 %copy.32 = bf16[1,5,256,1024]{3,2,1,0:T(8,128)(2,1)} copy(bf16[1,5,256,1024]{3,2,1,0:T(8,128)(2,1)} %bitcast.7) | data formatting | bytes 5242880
  180.3 0.0 copy-done
  180.3 0.0 copy-start.1
  180.3 0.8 copy.33
  181.2 0.0 copy-done.5
  181.2 0.6 copy.34
  181.8 0.0 copy-done.3
  181.8 0.7 copy.35
  182.4 0.0 copy-done.4
  182.4 0.6 copy.36
  183.1 0.0 copy-done.2
  183.1 0.8 copy.37
  183.9 0.0 copy-done.1
  183.9 0.8 copy.38
  (1 shorter events, 0.0 us)
Async XLA Ops:
  1.7 0.6 copy-start.6
  176.6 3.8 %copy-start = (bf16[5,64,1024]{2,1,0:T(8,128)(2,1)S(1)}, bf16[5,64,1024]{2,1,0:T(8,128)(2,1)}, u32[]{:S(2)}) copy-start(bf16[5,64,1024]{2,1,0:T(8,128)(2,1)} %get-tuple-element.21) | copy-start | bytes 1966084
  176.6 4.6 %copy-start.5 = (f32[32,512]{1,0:T(8,128)S(1)}, f32[32,512]{1,0:T(8,128)}, u32[]{:S(2)}) copy-start(f32[32,512]{1,0:T(8,128)} %get-tuple-element.45) | copy-start | bytes 196612
  176.6 5.2 %copy-start.3 = (f32[32,1024]{1,0:T(8,128)S(1)}, f32[32,1024]{1,0:T(8,128)}, u32[]{:S(2)}) copy-start(f32[32,1024]{1,0:T(8,128)} %get-tuple-element.46) | copy-start | bytes 393220
  176.6 5.9 %copy-start.4 = (f32[16,1024]{1,0:T(8,128)S(1)}, f32[16,1024]{1,0:T(8,128)}, u32[]{:S(2)}) copy-start(f32[16,1024]{1,0:T(8,128)} %get-tuple-element.47) | copy-start | bytes 196612
  176.6 6.5 %copy-start.2 = (f32[128,1024]{1,0:T(8,128)S(1)}, f32[128,1024]{1,0:T(8,128)}, u32[]{:S(2)}) copy-start(f32[128,1024]{1,0:T(8,128)} %get-tuple-element.48) | copy-start | bytes 1572868
  180.3 3.6 %copy-start.1 = (f32[1024,128]{1,0:T(8,128)S(1)}, f32[1024,128]{1,0:T(8,128)}, u32[]{:S(2)}) copy-start(f32[1024,128]{1,0:T(8,128)} %get-tuple-element.49) | copy-start | bytes 1572868

commit v3 on v2

--- a/solution.py
+++ b/solution.py
@@ -6,7 +6,6 @@
 from jax.sharding import PartitionSpec as P
 
 HEADS = 8
-FF_ROWS = 20
 
 
 def layer_norm(values, norm_gain, norm_shift):
@@ -391,6 +390,10 @@
     ydev = (img, yp * 2 + c)
     cdev = (img, y * 2 + cp)
     near = (1, 3, 2)
+    z1 = z + 1 - 2 * (z % 2)
+    z2 = (z + 2) % n_z
+    z3 = n_z - 1 - z
+    mid = jnp.logical_and(z >= 1, z <= 2)
 
     def zat(k):
         return (z + k) % n_z
@@ -401,7 +404,7 @@
     width = media_v.shape[2]
     slots = latent_v.shape[0]
     queries = latent_v.shape[1]
-    hidden = up_in.shape[2]
+    hidden = up_in.shape[1]
     inner = query_full.shape[3]
     f32 = jnp.float32
     bf16 = jnp.bfloat16
@@ -430,10 +433,15 @@
         pltpu.make_async_copy(query_in.at[0:16], slab.at[unit, 48:64, 0:inner], loc.at[2]),
         pltpu.make_async_copy(query_in.at[16:32], slab.at[unit, 48:64, inner:width], loc.at[3]),
         pltpu.make_async_copy(norm_in, normg.at[head, :, pl.ds(pl.multiple_of(img * 128, 128), 128)], loc.at[4]),
-        pltpu.make_async_copy(up_in, wide.at[pl.ds(img * 4, 4), :, 0:hidden], loc.at[5]),
+        pltpu.make_async_copy(up_in.at[:, 0:256], wide.at[0, img, :, 0:256], loc.at[5]),
         pltpu.make_async_copy(cot_in, pair.at[0:slots], loc.at[6]),
         pltpu.make_async_copy(latent_in, latent_v, loc.at[7]),
         pltpu.make_async_copy(media_in, media_v, loc.at[8]),
+    ] + [
+        pltpu.make_async_copy(
+            up_in.at[:, q * 256 : (q + 1) * 256], wide.at[q, img, :, 0:256], loc.at[8 + q]
+        )
+        for q in range(1, 4)
     ]
     for copy in local:
         copy.start()
@@ -456,18 +464,23 @@
     def put_slab(uu, sem, dev):
         send(slab.at[uu], slab.at[uu], sent.at[1], sem, dev)
 
-    for k in near:
-        put_slab(unit, at_z.at[z], zdev(zat(k)))
+    put_slab(unit, at_z.at[z], zdev(z2))
+    put_slab(unit, at_z.at[z], zdev(z1))
+
+    @pl.when(mid)
+    def _():
+        put_slab(unit, at_z.at[z], zdev(z3))
+
     put_slab(unit, at_x.at[z], xdev)
     put_slab(unit, at_y.at[img], ydev)
     put_slab(unit, at_c.at[img, y], cdev)
 
-    local[5].wait()
+    for copy in [local[5]] + local[9:12]:
+        copy.wait()
     down = down_in[...]
     for j in range(hidden // 128):
-        wide[pl.ds(img * 4, 4), :, hidden + j * 128 : hidden + (j + 1) * 128] = tpose(
-            down[j * 128 : (j + 1) * 128, :]
-        ).reshape(4, 32, 128)
+        at = 256 + (j % 2) * 128
+        wide[j // 2, img, :, at : at + 128] = tpose(down[j * 128 : (j + 1) * 128, :])
 
     local[6].wait()
     filled = counts[0]
@@ -486,16 +499,20 @@
         ii = zz * n_x + x
         send(normg.at[head, :, lanes(ii)], normg.at[head, :, lanes(ii)], sent.at[2], nb_x.at[zz], xdev)
 
-    def at_forward_z(k):
-        zz = zat(k)
+    def at_forward_z(zz, onward):
         uu = (zz * n_x + x) * n_head + head
         arrived(slab.at[uu], at_z.at[zz])
+        if onward:
+
+            @pl.when(mid)
+            def _():
+                put_slab(uu, at_z.at[zz], zdev(z1))
+
         put_slab(uu, at_x.at[zz], xdev)
         put_slab(uu, at_y.at[zz * n_x + x], ydev)
         put_slab(uu, at_c.at[zz * n_x + x, y], cdev)
 
-    def at_forward_x(k):
-        zz = zat(k)
+    def at_forward_x(zz):
         ii = zz * n_x + xp
         uu = ii * n_head + head
         arrived(slab.at[uu], at_x.at[zz])
@@ -507,29 +524,55 @@
         arrived(slab.at[uu], at_y.at[ii])
         put_slab(uu, at_c.at[ii, yp], cdev)
 
-    at_forward_z(1)
-    at_forward_x(0)
-    at_forward_z(3)
+    at_forward_z(z2, True)
+    at_forward_x(z)
+    at_forward_z(z1, False)
     for k in (0,) + near:
         zz = zat(k)
         arrived(normg.at[head, :, lanes(zz * n_x + xp)], nb_x.at[zz])
     send(normg.at[head], normg.at[head], sent.at[3], nb_y.at[0], ydev)
     send(normg.at[head], normg.at[head], sent.at[4], nb_c.at[y], cdev)
-    at_forward_z(2)
-
-    def ff_unit(ii, q):
-        return wide.at[ii * 4 + q]
-
-    for q in range(4):
-        for k in near:
-            send(ff_unit(img, q), ff_unit(img, q), sent.at[5], ff_z.at[z, q], zdev(zat(k)))
-    at_forward_x(1)
+    at_forward_z(z3, False)
+
+    def ff_unit(q, ii):
+        return wide.at[q, ii]
+
+    def ff_own_z(q):
+        piece = ff_unit(q, img)
+        send(piece, piece, sent.at[5], ff_z.at[z, q], zdev(z2))
+        send(piece, piece, sent.at[5], ff_z.at[z, q], zdev(z1))
+
+        @pl.when(mid)
+        def _():
+            send(piece, piece, sent.at[5], ff_z.at[z, q], zdev(z3))
+
+    def ff_own_x(q):
+        piece = ff_unit(q, img)
+        send(piece, piece, sent.at[6], ff_x.at[z, q], xdev)
+
+    def ff_forward(q):
+        for zz in (z2, z1, z3):
+            piece = ff_unit(q, zz * n_x + x)
+            arrived(piece, ff_z.at[zz, q])
+            if zz is z2:
+
+                @pl.when(mid)
+                def _():
+                    send(piece, piece, sent.at[5], ff_z.at[zz, q], zdev(z1))
+
+            send(piece, piece, sent.at[6], ff_x.at[zz, q], xdev)
+        if q + 2 < 4:
+            ff_own_z(q + 2)
+            ff_own_x(q + 2)
+
+    for q in range(2):
+        ff_own_z(q)
+        ff_own_x(q)
+    at_forward_x(z2)
     arrived(normg.at[yp * 2 + c], nb_y.at[0])
     send(normg.at[yp * 2 + c], normg.at[yp * 2 + c], sent.at[4], nb_c.at[yp], cdev)
-    at_forward_x(3)
-    for q in range(4):
-        send(ff_unit(img, q), ff_unit(img, q), sent.at[6], ff_x.at[z, q], xdev)
-    at_forward_x(2)
+    at_forward_x(z1)
+    at_forward_x(z3)
     own_cot = cotr.at[pl.ds(head * slots, slots)]
     send(own_cot, own_cot, sent.at[7], bg_y.at[0], ydev)
     send(own_cot, own_cot, sent.at[7], bg_c.at[y], cdev)
@@ -569,11 +612,11 @@
     local[7].wait()
     lax.fori_loop(0, slots, norm_latent, 0)
     at_forward_y(img)
-    at_forward_y(zat(1) * n_x + x)
+    at_forward_y(z2 * n_x + x)
     local[8].wait()
     blocks = media_v.shape[0]
     step = blocks // 4
-    order = [z * n_x + xp, zat(3) * n_x + x, zat(2) * n_x + x, zat(1) * n_x + xp, zat(3) * n_x + xp, zat(2) * n_x + xp]
+    order = [z * n_x + xp, z1 * n_x + x, z3 * n_x + x, z2 * n_x + xp, z1 * n_x + xp, z3 * n_x + xp]
     for r in range(4):
         lax.fori_loop(r * step, (r + 1) * step, norm_media, 0)
         at_forward_y(order[r])
@@ -600,23 +643,12 @@
     turn_latent(latent_n, latent_t, width)
     at_forward_y(order[4])
     lax.fori_loop(0, blocks * queries // 128, turn_media, 0)
+    ff_forward(0)
     at_forward_y(order[5])
 
-    def ff_forward(e):
-        q = e // 3
-        step_k = e % 3
-        kk = step_k + 1
-        zz = (z + kk) % n_z
-        piece = ff_unit(zz * n_x + x, q)
-        arrived(piece, ff_z.at[zz, q])
-        send(piece, piece, sent.at[6], ff_x.at[zz, q], xdev)
-
-    for e in range(3):
-        ff_forward(e)
     for ii in range(8):
         for yy in range(2):
             arrived(slab.at[ii * n_head + yy * 2 + cp], at_c.at[ii, yy])
-    ff_forward(3)
 
     query_full[:, 0] = slab[:, 48:64, 0:inner]
     query_full[:, 1] = slab[:, 48:64, inner:width]
@@ -649,8 +681,9 @@
         kv_media[:, :, tile(t)] = dot_nn(media_rows_n, weight).astype(bf16).reshape(groups, 256, 256)
         return carry
 
-    lax.fori_loop(0, width // 256, kv_step, 0)
-    ff_forward(4)
+    lax.fori_loop(0, width // 512, kv_step, 0)
+    ff_forward(1)
+    lax.fori_loop(width // 512, width // 256, kv_step, 0)
 
     def lane_mask(hh, dtype):
         lane = lax.broadcasted_iota(jnp.int32, (1, 256), 1)
@@ -697,17 +730,17 @@
         piece = hid.at[head * slots + m]
         send(piece, piece, sent.at[8], hd_y.at[m], ydev)
         send(piece, piece, sent.at[8], hd_c.at[m], cdev)
-        ff_forward(m + 5)
-        return carry
-
-    lax.fori_loop(0, slots, forward_image, 0)
+        return carry
+
+    lax.fori_loop(0, 2, forward_image, 0)
+    ff_forward(2)
+    lax.fori_loop(2, slots, forward_image, 0)
 
     other = yp * 2 + c
     cot_other = cotr.at[pl.ds(other * slots, slots)]
     arrived(cot_other, bg_y.at[0])
     send(cot_other, cot_other, sent.at[7], bg_c.at[yp], cdev)
     turn_latent(att_v, att_t, inner)
-    ff_forward(10)
     for yy in (y, yp):
         arrived(cotr.at[pl.ds((yy * 2 + cp) * slots, slots)], bg_c.at[yy])
 
@@ -725,7 +758,34 @@
         lax.fori_loop(0, all_rows // 128, body, 0)
 
     turn_rows(cotr, 1)
-    ff_forward(11)
+    ff_forward(3)
+
+    act_at = 4 * slots
+
+    def ff_rows(q, start):
+        rows = pl.ds(start, 2 * slots)
+        pre = dot_nn(hid[rows].reshape(all_rows // 2, width), wide[q, :, :, 0:256].reshape(width, 256))
+        grad = dot_nn(cotr[rows].reshape(all_rows // 2, width), wide[q, :, :, 256:512].reshape(width, 256))
+        below = 0.5 * (1.0 + lax.erf(pre * 0.7071067811865476))
+        slope = below + pre * (jnp.exp(-0.5 * pre * pre) * 0.3989422804014327)
+        pair[rows, :, tile(q)] = (grad * slope).astype(bf16).reshape(2 * slots, queries, 256)
+        pair[pl.ds(act_at + start, 2 * slots), :, tile(q)] = (
+            (pre * below).astype(bf16).reshape(2 * slots, queries, 256)
+        )
+
+    def ff_near(q, carry):
+        for zz in range(n_z):
+            arrived(ff_unit(q, zz * n_x + xp), ff_x.at[zz, q])
+        ff_rows(q, y * 2 * slots)
+        return carry
+
+    def ff_far(q, carry):
+        ff_rows(q, yp * 2 * slots)
+        return carry
+
+    def hid_near(m, carry):
+        arrived(hid.at[(y * 2 + cp) * slots + m], hd_c.at[m])
+        return carry
 
     def hid_forward(m, carry):
         piece = hid.at[other * slots + m]
@@ -733,54 +793,42 @@
         send(piece, piece, sent.at[8], hd_f.at[m], cdev)
         return carry
 
+    def hid_far(m, carry):
+        arrived(hid.at[(yp * 2 + cp) * slots + m], hd_f.at[m])
+        return carry
+
+    def grad_tile(q, carry):
+        def over_parts(part, carry2):
+            right = pair[pl.ds(part * act_at, act_at), :, tile(q)].reshape(all_rows, 256)
+            value = dot_nn(turned[part], right).astype(bf16).reshape(n_z, n_x, 128, 256)
+            grads[q, part, 0] = value[:, 0]
+            grads[q, part, 1] = value[:, 1]
+            send(grads.at[q, part, xp], xrecv.at[q, part], sent.at[11], rf_x.at[q, part], xdev)
+            return carry2
+
+        return lax.fori_loop(0, 2, over_parts, carry)
+
+    lax.fori_loop(0, slots, hid_near, 0)
+    lax.fori_loop(0, 3, ff_near, 0)
     lax.fori_loop(0, slots, hid_forward, 0)
-
-    def hid_arrived(m, carry):
-        arrived(hid.at[(y * 2 + cp) * slots + m], hd_c.at[m])
-        arrived(hid.at[(yp * 2 + cp) * slots + m], hd_f.at[m])
-        return carry
-
-    lax.fori_loop(0, slots, hid_arrived, 0)
+    lax.fori_loop(0, slots, hid_far, 0)
     turn_rows(hid, 0)
-
-    def ff_arrived(e, carry):
-        zz = e // 4
-        q = e % 4
-        arrived(ff_unit(zz * n_x + xp, q), ff_x.at[zz, q])
-        return carry
-
-    lax.fori_loop(0, 16, ff_arrived, 0)
-
-    act_at = 4 * slots
-
-    def wide_tile(start):
-        return wide[:, :, pl.ds(pl.multiple_of(start, 256), 256)].reshape(width, 256)
-
-    def ff_step(t, carry):
-        up = wide_tile(t * 256)
-        dn = wide_tile(hidden + t * 256)
-
-        def over_rows(r, carry2):
-            rows = pl.ds(r * FF_ROWS, FF_ROWS)
-            pre = dot_nn(hid[rows].reshape(FF_ROWS * 64, width), up)
-            grad = dot_nn(cotr[rows].reshape(FF_ROWS * 64, width), dn)
-            below = 0.5 * (1.0 + lax.erf(pre * 0.7071067811865476))
-            slope = below + pre * (jnp.exp(-0.5 * pre * pre) * 0.3989422804014327)
-            pair[rows, :, tile(t)] = (grad * slope).astype(bf16).reshape(FF_ROWS, 64, 256)
-            pair[pl.ds(act_at + r * FF_ROWS, FF_ROWS), :, tile(t)] = (
-                (pre * below).astype(bf16).reshape(FF_ROWS, 64, 256)
-            )
-            return carry2
-
-        return lax.fori_loop(0, act_at // FF_ROWS, over_rows, carry)
-
-    lax.fori_loop(0, hidden // 256, ff_step, 0)
-
-    def wide_rows(part, t):
-        return wide[pl.ds(t * 16, 16), :, part * hidden : (part + 1) * hidden].reshape(512, hidden)
+    ff_far(0, 0)
+    grad_tile(0, 0)
+    ff_near(3, 0)
+    lax.fori_loop(1, 4, ff_far, 0)
+
+    def wide_rows(part, q, t):
+        return wide[q, pl.ds(t * 4, 4), :, part * 256 : (part + 1) * 256].reshape(512, 256)
 
     def broad(t):
         return pl.ds(pl.multiple_of(t * 512, 512), 512)
+
+    def back_rows(left, part, t):
+        total = contract_cols(left[:, 0:256], wide_rows(part, 0, t))
+        for q in range(1, 4):
+            total = total + contract_cols(left[:, q * 256 : (q + 1) * 256], wide_rows(part, q, t))
+        return total
 
     def head_sum(part):
         def rows_of(hh):
@@ -790,17 +838,17 @@
             left = rows_of(hh)
 
             def to_core(t, carry, left=left, slot=slot):
-                value = contract_cols(left, wide_rows(part, t))
-                hsend[part, slot, :, :, broad(t)] = value.astype(bf16).reshape(slots, queries, 512)
+                value = back_rows(left, part, t)
+                hsend[slot, :, :, broad(t)] = value.astype(bf16).reshape(slots, queries, 512)
                 return carry
 
             lax.fori_loop(0, width // 512, to_core, 0)
-            send(hsend.at[part, slot], hrecv.at[part, slot], sent.at[9], hp_c.at[part, slot], cdev)
+            send(hsend.at[slot], hrecv.at[part, slot], sent.at[9], hp_c.at[part, slot], cdev)
         left_y = rows_of(yp * 2 + c)
         arrived(hrecv.at[part, 0], hp_c.at[part, 0])
 
         def to_y(t, carry):
-            value = contract_cols(left_y, wide_rows(part, t)).reshape(slots, queries, 512)
+            value = back_rows(left_y, part, t).reshape(slots, queries, 512)
             hysend[part, :, :, broad(t)] = (value + hrecv[part, 0, :, :, broad(t)].astype(f32)).astype(bf16)
             return carry
 
@@ -810,7 +858,7 @@
         arrived(hrecv.at[part, 1], hp_c.at[part, 1])
 
         def to_own(t, carry):
-            value = contract_cols(left_own, wide_rows(part, t)).reshape(slots, queries, 512)
+            value = back_rows(left_own, part, t).reshape(slots, queries, 512)
             hown[part, :, :, broad(t)] = value + hrecv[part, 1, :, :, broad(t)].astype(f32)
             return carry
 
@@ -819,42 +867,21 @@
     arrived(hid.at[0 : 3 * slots], sent.at[8])
     head_sum(0)
 
-    def grad_unit(u, carry):
-        zz = (z + 1 + u // 2) % n_z
-        part = u % 2
-        left = turned[part, pl.ds(pl.multiple_of(zz * 256, 256), 256), :]
-
-        right = pair[pl.ds(part * act_at, act_at)].reshape(all_rows, hidden)
-        value = dot_nn(left, right).astype(bf16).reshape(2, 128, hidden)
-        grads[zz, 0, part] = value[0]
-        grads[zz, 1, part] = value[1]
-        send(grads.at[zz, xp, part], xrecv.at[zz, part], sent.at[11], rf_x.at[zz, part], xdev)
-        return carry
-
-    def sum_unit(u):
-        zz = (z + 1 + u // 2) % n_z
-        part = u % 2
-        arrived(xrecv.at[zz, part], rf_x.at[zz, part])
-
-        def over(r, carry2):
-            rows = pl.ds(pl.multiple_of(r * 16, 16), 16)
-            grads[zz, x, part, rows, :] = (
-                grads[zz, x, part, rows, :].astype(f32) + xrecv[zz, part, rows, :].astype(f32)
+    def sum_tile(u):
+        q, part = u // 2, u % 2
+        arrived(xrecv.at[q, part], rf_x.at[q, part])
+        for k, zz in enumerate((z1, z2, z3)):
+            grads[q, part, x, zz] = (
+                grads[q, part, x, zz].astype(f32) + xrecv[q, part, zz].astype(f32)
             ).astype(bf16)
-            return carry2
-
-        lax.fori_loop(0, 8, over, 0)
-        send(grads.at[zz, x, part], zrecv.at[z, part], sent.at[12], rf_z.at[z, part], zdev(zz))
-
-    def grad_and_sum(u, carry):
-        grad_unit(u, carry)
-        sum_unit(u - 4)
-        return carry
-
-    lax.fori_loop(0, 4, grad_unit, 0)
-    lax.fori_loop(4, 8, grad_and_sum, 0)
+            send(grads.at[q, part, x, zz], zrecv.at[k, part, q], sent.at[12], rf_z.at[k, part], zdev(zz))
+
+    lax.fori_loop(1, 4, grad_tile, 0)
+    sum_tile(0)
+    sum_tile(1)
+    arrived(hsend, sent.at[9])
     head_sum(1)
-    sum_unit(4)
+    sum_tile(2)
 
     gacc[...] = jnp.zeros_like(gacc)
 
@@ -870,6 +897,7 @@
             g - jnp.mean(g, axis=-1, keepdims=True) - xhat * jnp.mean(g * xhat, axis=-1, keepdims=True)
         )
 
+    sum_tile(3)
     arrived(hyrecv.at[0], hp_y.at[0])
 
     def mid_back(m, carry):
@@ -902,7 +930,7 @@
         return carry
 
     lax.fori_loop(0, width // 512, out_grad_step, 0)
-    sum_unit(5)
+    sum_tile(4)
 
     def back_pair(m, g):
         q_rows, k_media, k_latent, p_media, p_latent = probabilities(m, g)
@@ -928,6 +956,8 @@
         return carry
 
     lax.fori_loop(0, slots, back_image, 0)
+
+    sum_tile(5)
 
     gcr = hid
     gyr_v = media_n
@@ -999,6 +1029,7 @@
     stage_y(chunk[1])
     kv_grad_chunk(chunk[3])
     stage_y(chunk[2])
+    sum_tile(6)
 
     arrived(hyrecv.at[1], hp_y.at[1])
     new_v = delta_v
@@ -1045,6 +1076,7 @@
     latent_copy = pltpu.make_async_copy(latent_v, latent_out, outs.at[2])
     latent_copy.start()
     lax.fori_loop(0, 2, media_back, 0)
+    sum_tile(7)
     stage_x(chunk[0])
     stage_x(chunk[1])
     lax.fori_loop(2, 4, media_back, 0)
@@ -1078,29 +1110,24 @@
     norm_out[...] = total
 
     for part in range(2):
-        arrived(xrecv.at[z, part], rf_x.at[z, part])
-        for k in near:
-            arrived(zrecv.at[zat(k), part], rf_z.at[zat(k), part])
-
-    def up_last(r, carry):
-        rows = pl.ds(pl.multiple_of(r * 16, 16), 16)
-        value = grads[z, x, 0, rows, :].astype(f32) + xrecv[z, 0, rows, :].astype(f32)
-        for k in near:
-            value = value + zrecv[zat(k), 0, rows, :].astype(f32)
-        up_out[rows, :] = value
-        return carry
-
-    lax.fori_loop(0, 8, up_last, 0)
-
-    def down_last(j, carry):
-        cols = pl.ds(pl.multiple_of(j * 128, 128), 128)
-        value = grads[z, x, 1, :, cols].astype(f32) + xrecv[z, 1, :, cols].astype(f32)
-        for k in near:
-            value = value + zrecv[zat(k), 1, :, cols].astype(f32)
-        down_out[cols, :] = tpose(value)
-        return carry
-
-    lax.fori_loop(0, hidden // 128, down_last, 0)
+        for k in range(3):
+            arrived(zrecv.at[k, part], rf_z.at[k, part])
+
+    def own_sum(part, q):
+        value = grads[q, part, x, z].astype(f32) + xrecv[q, part, z].astype(f32)
+        for k in range(3):
+            value = value + zrecv[k, part, q].astype(f32)
+        return value
+
+    def last_sums(q, carry):
+        up_out[:, tile(q)] = own_sum(0, q)
+        value = own_sum(1, q)
+        for j in range(2):
+            rows = pl.ds(pl.multiple_of(q * 256 + j * 128, 128), 128)
+            down_out[rows, :] = tpose(value[:, j * 128 : (j + 1) * 128])
+        return carry
+
+    lax.fori_loop(0, hidden // 256, last_sums, 0)
 
     final = stage_z(chunk[3], True)
     for k in near:
@@ -1116,17 +1143,23 @@
     latent_copy.wait()
     arrived(media_v, outs.at[1])
     arrived(normg.at[0, :, 0:384], sent.at[0])
-    arrived(slab.at[0:31], sent.at[1])
+    arrived(slab.at[0:30], sent.at[1])
+
+    @pl.when(mid)
+    def _():
+        arrived(slab.at[0:2], sent.at[1])
+        arrived(wide.at[0], sent.at[5])
+
     arrived(normg.at[0, :, 0:512], sent.at[2])
     arrived(normg.at[0], sent.at[3])
     arrived(normg.at[0:2], sent.at[4])
-    arrived(wide.at[0:12], sent.at[5])
-    arrived(wide.at[0:16], sent.at[6])
+    arrived(wide.at[0], sent.at[5])
+    arrived(wide.at[0:2], sent.at[6])
     arrived(cotr.at[0 : 3 * slots], sent.at[7])
     arrived(hsend, sent.at[9])
     arrived(hysend, sent.at[10])
     arrived(xrecv, sent.at[11])
-    arrived(zrecv.at[0:3], sent.at[12])
+    arrived(zrecv, sent.at[12])
     arrived(gcr.at[0:16], sent.at[13])
     arrived(gyr_v.at[0:8], sent.at[14])
     arrived(gyr_v.at[0:4], sent.at[15])
@@ -1186,7 +1219,7 @@
         scratch_shapes=[
             pltpu.VMEM((32, 64, width), bf16),
             pltpu.VMEM((32, 2, 16, inner), bf16),
-            pltpu.VMEM((32, 32, 2 * hidden), bf16),
+            pltpu.VMEM((4, 8, rows_up, 512), bf16),
             pltpu.VMEM((4 * slots, queries, width), bf16),
             pltpu.VMEM((4 * slots, queries, width), bf16),
             pltpu.VMEM((2, width, all_rows), bf16),
@@ -1203,10 +1236,10 @@
             pltpu.VMEM((inner, rows_latent), bf16),
             pltpu.VMEM((slots, queries, width), f32),
             pltpu.VMEM((8 * slots, queries, width), bf16),
-            pltpu.VMEM((4, 2, 2, rows_up, hidden), bf16),
-            pltpu.VMEM((4, 2, rows_up, hidden), bf16),
-            pltpu.VMEM((4, 2, rows_up, hidden), bf16),
-            pltpu.VMEM((2, 2, slots, queries, width), bf16),
+            pltpu.VMEM((4, 2, 2, 4, rows_up, 256), bf16),
+            pltpu.VMEM((4, 2, 4, rows_up, 256), bf16),
+            pltpu.VMEM((3, 2, 4, rows_up, 256), bf16),
+            pltpu.VMEM((2, slots, queries, width), bf16),
             pltpu.VMEM((2, 2, slots, queries, width), bf16),
             pltpu.VMEM((2, slots, queries, width), bf16),
             pltpu.VMEM((2, slots, queries, width), bf16),
@@ -1221,7 +1254,7 @@
             pltpu.VMEM((3, 8, width), f32),
             pltpu.VMEM((4, 8, 128), f32),
             pltpu.VMEM((4, 64, width), bf16),
-            dma((9,)),
+            dma((12,)),
             dma((4,)),
             dma((4,)),
             dma((8,)),
@@ -1261,7 +1294,7 @@
         query_weight,
         key_value_weight,
         output_weight,
-        up_weight.reshape(4, rows_up // 4, hidden),
+        up_weight,
         down_weight,
         norm_tile,
     )

time: 185 us -> 167 us (0.903)
  Pallas kernels: 170 us -> 152 us
    pallas_call x1, Pallas kernels: 170 us -> 152 us  [block_plan(): pl.pallas_call(block_kernel, out_shape=(shape((slots, queries, width), bf...]
where the time goes in v3:
time: 167 us; the launch traced here: 166 us
  Pallas kernels  152 us (91%)
  local copies, waits for them, and re-layouts  12.4 us (7%)
    pallas_call x1, Pallas kernels, block_plan(): pl.pallas_call(block_kernel, out_shape=(shape((slots, queries, width), bf...  152 us
    unnamed x22, local copies, waits for them, and re-layouts  10.7 us

profile of v3, /device:TPU:0, one launch (start us, length us, event | category | flops | bytes accessed | tf_op | source)
XLA Modules:
  0.0 166.4 jit_solution(5751258285268602225)
XLA Ops:
  0.6 0.7 maximum_convert_fusion
  1.4 0.4 dynamic_update_slice.3.norm_in
  1.7 0.0 copy-start.6
  1.8 0.6 copy-done.6
  3.0 152.0 %shard_map.186 = (bf16[5,64,1024]{2,1,0:T(8,128)(2,1)}, bf16[20,64,1024]{2,1,0:T(8,128)(2,1)}, bf16[5,64,1024]{2,1,0:T(8,128)(2,1)}, f32[8,128]{1,0:T(8,128)}, f...) custom-call(s32[1]{0:T(128)S(6)} %copy.30.counts, ...), custom_call_target="tpu_custom_call" | custom-call | tf_op jit(solution)/shard_map/pallas_call | solution.py:1204
  155.0 0.8 constant_dynamic-slice_fusion
  155.7 0.6 fusion
  156.3 2.0 %copy.31 = bf16[1,5,64,1024]{3,2,1,0:T(8,128)(2,1)} copy(bf16[1,5,64,1024]{3,2,1,0:T(8,128)(2,1)} %bitcast.9) | data formatting | bytes 1310720
  158.3 0.0 copy-start
  158.3 0.0 copy-start.5
  158.3 0.0 copy-start.3
  158.3 0.0 copy-start.4
  158.3 0.0 copy-start.2
  158.3 3.7 %copy.32 = bf16[1,5,256,1024]{3,2,1,0:T(8,128)(2,1)} copy(bf16[1,5,256,1024]{3,2,1,0:T(8,128)(2,1)} %bitcast.6) | data formatting | bytes 5242880
  162.0 0.0 copy-done
  162.1 0.0 copy-start.1
  162.1 0.8 copy.33
  162.9 0.0 copy-done.5
  162.9 0.6 copy.34
  163.5 0.0 copy-done.3
  163.5 0.7 copy.35
  164.2 0.0 copy-done.4
  164.2 0.6 copy.36
  164.8 0.0 copy-done.2
  164.8 0.8 copy.37
  165.6 0.0 copy-done.1
  165.6 0.8 copy.38
  (1 shorter events, 0.0 us)
Async XLA Ops:
  1.7 0.6 copy-start.6
  158.3 3.8 %copy-start = (bf16[5,64,1024]{2,1,0:T(8,128)(2,1)S(1)}, bf16[5,64,1024]{2,1,0:T(8,128)(2,1)}, u32[]{:S(2)}) copy-start(bf16[5,64,1024]{2,1,0:T(8,128)(2,1)} %get-tuple-element.21) | copy-start | bytes 1966084
  158.3 4.6 %copy-start.5 = (f32[32,512]{1,0:T(8,128)S(1)}, f32[32,512]{1,0:T(8,128)}, u32[]{:S(2)}) copy-start(f32[32,512]{1,0:T(8,128)} %get-tuple-element.45) | copy-start | bytes 196612
  158.3 5.2 %copy-start.3 = (f32[32,1024]{1,0:T(8,128)S(1)}, f32[32,1024]{1,0:T(8,128)}, u32[]{:S(2)}) copy-start(f32[32,1024]{1,0:T(8,128)} %get-tuple-element.46) | copy-start | bytes 393220
  158.3 5.9 %copy-start.4 = (f32[16,1024]{1,0:T(8,128)S(1)}, f32[16,1024]{1,0:T(8,128)}, u32[]{:S(2)}) copy-start(f32[16,1024]{1,0:T(8,128)} %get-tuple-element.47) | copy-start | bytes 196612
  158.3 6.5 %copy-start.2 = (f32[128,1024]{1,0:T(8,128)S(1)}, f32[128,1024]{1,0:T(8,128)}, u32[]{:S(2)}) copy-start(f32[128,1024]{1,0:T(8,128)} %get-tuple-element.48) | copy-start | bytes 1572868
  162.1 3.6 %copy-start.1 = (f32[1024,128]{1,0:T(8,128)S(1)}, f32[1024,128]{1,0:T(8,128)}, u32[]{:S(2)}) copy-start(f32[1024,128]{1,0:T(8,128)} %get-tuple-element.49) | copy-start | bytes 1572868

commit v4 on v3

--- a/solution.py
+++ b/solution.py
@@ -302,7 +302,8 @@
     output_in,
     up_in,
     down_in,
-    norm_in,
+    gain_in,
+    bias_in,
     new_out,
     media_out,
     latent_out,
@@ -432,14 +433,13 @@
         pltpu.make_async_copy(output_in, slab.at[unit, 32:48], loc.at[1]),
         pltpu.make_async_copy(query_in.at[0:16], slab.at[unit, 48:64, 0:inner], loc.at[2]),
         pltpu.make_async_copy(query_in.at[16:32], slab.at[unit, 48:64, inner:width], loc.at[3]),
-        pltpu.make_async_copy(norm_in, normg.at[head, :, pl.ds(pl.multiple_of(img * 128, 128), 128)], loc.at[4]),
-        pltpu.make_async_copy(up_in.at[:, 0:256], wide.at[0, img, :, 0:256], loc.at[5]),
-        pltpu.make_async_copy(cot_in, pair.at[0:slots], loc.at[6]),
-        pltpu.make_async_copy(latent_in, latent_v, loc.at[7]),
-        pltpu.make_async_copy(media_in, media_v, loc.at[8]),
+        pltpu.make_async_copy(up_in.at[:, 0:256], wide.at[0, img, :, 0:256], loc.at[4]),
+        pltpu.make_async_copy(cot_in, pair.at[0:slots], loc.at[5]),
+        pltpu.make_async_copy(latent_in, latent_v, loc.at[6]),
+        pltpu.make_async_copy(media_in, media_v, loc.at[7]),
     ] + [
         pltpu.make_async_copy(
-            up_in.at[:, q * 256 : (q + 1) * 256], wide.at[q, img, :, 0:256], loc.at[8 + q]
+            up_in.at[:, q * 256 : (q + 1) * 256], wide.at[q, img, :, 0:256], loc.at[7 + q]
         )
         for q in range(1, 4)
     ]
@@ -455,34 +455,46 @@
     def lanes(ii):
         return pl.ds(pl.multiple_of(ii * 128, 128), 128)
 
-    local[4].wait()
+    part = gain_in.shape[1]
+    norm_own = normg.at[head, :, lanes(img)]
+    normv[:, 0:128] = jnp.zeros((8, 128), f32)
+    normv[0:3, 0:part] = gain_in[...].astype(f32)
+    normv[3:6, 0:part] = bias_in[...].astype(f32)
+    norm_own[...] = pltpu.roll(normv[:, 0:128], head * part, 1)
     for k in near:
-        send(norm_in, normg.at[head, :, lanes(img)], sent.at[0], nb_z.at[z], zdev(zat(k)))
+        send(norm_own, norm_own, sent.at[0], nb_z.at[z], zdev(zat(k)))
     for copy in local[0:4]:
         copy.wait()
 
     def put_slab(uu, sem, dev):
         send(slab.at[uu], slab.at[uu], sent.at[1], sem, dev)
 
-    put_slab(unit, at_z.at[z], zdev(z2))
-    put_slab(unit, at_z.at[z], zdev(z1))
-
-    @pl.when(mid)
-    def _():
-        put_slab(unit, at_z.at[z], zdev(z3))
-
-    put_slab(unit, at_x.at[z], xdev)
-    put_slab(unit, at_y.at[img], ydev)
-    put_slab(unit, at_c.at[img, y], cdev)
-
-    for copy in [local[5]] + local[9:12]:
+    def put_line(ii):
+        uu = ii * n_head + head
+        put_slab(uu, at_z.at[z, ii % n_x], zdev(z2))
+        put_slab(uu, at_z.at[z, ii % n_x], zdev(z1))
+
+        @pl.when(mid)
+        def _():
+            put_slab(uu, at_z.at[z, ii % n_x], zdev(z3))
+
+    def put_chip(ii):
+        uu = ii * n_head + head
+        put_slab(uu, at_y.at[ii], ydev)
+        put_slab(uu, at_c.at[ii, y], cdev)
+
+    put_slab(unit, at_x.at[0], xdev)
+    put_line(img)
+    put_chip(img)
+
+    for copy in [local[4]] + local[8:11]:
         copy.wait()
     down = down_in[...]
     for j in range(hidden // 128):
         at = 256 + (j % 2) * 128
         wide[j // 2, img, :, at : at + 128] = tpose(down[j * 128 : (j + 1) * 128, :])
 
-    local[6].wait()
+    local[5].wait()
     filled = counts[0]
     for m in range(slots):
         keep = jnp.clip(filled - m, 0, 1).astype(f32)
@@ -499,83 +511,76 @@
         ii = zz * n_x + x
         send(normg.at[head, :, lanes(ii)], normg.at[head, :, lanes(ii)], sent.at[2], nb_x.at[zz], xdev)
 
-    def at_forward_z(zz, onward):
-        uu = (zz * n_x + x) * n_head + head
-        arrived(slab.at[uu], at_z.at[zz])
+    def at_forward_x():
+        ii = z * n_x + xp
+        arrived(slab.at[ii * n_head + head], at_x.at[0])
+        put_line(ii)
+        put_chip(ii)
+
+    def at_forward_z(zz, xx, onward):
+        ii = zz * n_x + xx
+        uu = ii * n_head + head
+        arrived(slab.at[uu], at_z.at[zz, xx])
         if onward:
 
             @pl.when(mid)
             def _():
-                put_slab(uu, at_z.at[zz], zdev(z1))
-
-        put_slab(uu, at_x.at[zz], xdev)
-        put_slab(uu, at_y.at[zz * n_x + x], ydev)
-        put_slab(uu, at_c.at[zz * n_x + x, y], cdev)
-
-    def at_forward_x(zz):
-        ii = zz * n_x + xp
-        uu = ii * n_head + head
-        arrived(slab.at[uu], at_x.at[zz])
-        put_slab(uu, at_y.at[ii], ydev)
-        put_slab(uu, at_c.at[ii, y], cdev)
+                put_slab(uu, at_z.at[zz, xx], zdev(z1))
+
+        put_chip(ii)
 
     def at_forward_y(ii):
         uu = ii * n_head + yp * 2 + c
         arrived(slab.at[uu], at_y.at[ii])
         put_slab(uu, at_c.at[ii, yp], cdev)
 
-    at_forward_z(z2, True)
-    at_forward_x(z)
-    at_forward_z(z1, False)
+    def ff_unit(q, ii):
+        return wide.at[q, ii]
+
+    def ff_own_z(q):
+        piece = ff_unit(q, img)
+        send(piece, piece, sent.at[5], ff_z.at[z, q], zdev(z2))
+        send(piece, piece, sent.at[5], ff_z.at[z, q], zdev(z1))
+
+        @pl.when(mid)
+        def _():
+            send(piece, piece, sent.at[5], ff_z.at[z, q], zdev(z3))
+
+    def ff_own_x(q):
+        piece = ff_unit(q, img)
+        send(piece, piece, sent.at[6], ff_x.at[z, q], xdev)
+
+    def ff_forward(q):
+        for zz in (z2, z1, z3):
+            piece = ff_unit(q, zz * n_x + x)
+            arrived(piece, ff_z.at[zz, q])
+            if zz is z2:
+
+                @pl.when(mid)
+                def _():
+                    send(piece, piece, sent.at[5], ff_z.at[zz, q], zdev(z1))
+
+            send(piece, piece, sent.at[6], ff_x.at[zz, q], xdev)
+        if q + 2 < 4:
+            ff_own_z(q + 2)
+
+    for q in range(4):
+        ff_own_x(q)
+    at_forward_x()
     for k in (0,) + near:
         zz = zat(k)
         arrived(normg.at[head, :, lanes(zz * n_x + xp)], nb_x.at[zz])
     send(normg.at[head], normg.at[head], sent.at[3], nb_y.at[0], ydev)
     send(normg.at[head], normg.at[head], sent.at[4], nb_c.at[y], cdev)
-    at_forward_z(z3, False)
-
-    def ff_unit(q, ii):
-        return wide.at[q, ii]
-
-    def ff_own_z(q):
-        piece = ff_unit(q, img)
-        send(piece, piece, sent.at[5], ff_z.at[z, q], zdev(z2))
-        send(piece, piece, sent.at[5], ff_z.at[z, q], zdev(z1))
-
-        @pl.when(mid)
-        def _():
-            send(piece, piece, sent.at[5], ff_z.at[z, q], zdev(z3))
-
-    def ff_own_x(q):
-        piece = ff_unit(q, img)
-        send(piece, piece, sent.at[6], ff_x.at[z, q], xdev)
-
-    def ff_forward(q):
-        for zz in (z2, z1, z3):
-            piece = ff_unit(q, zz * n_x + x)
-            arrived(piece, ff_z.at[zz, q])
-            if zz is z2:
-
-                @pl.when(mid)
-                def _():
-                    send(piece, piece, sent.at[5], ff_z.at[zz, q], zdev(z1))
-
-            send(piece, piece, sent.at[6], ff_x.at[zz, q], xdev)
-        if q + 2 < 4:
-            ff_own_z(q + 2)
-            ff_own_x(q + 2)
-
+    at_forward_z(z2, x, True)
+    at_forward_z(z1, x, False)
+    at_forward_z(z3, x, False)
+    arrived(normg.at[yp * 2 + c], nb_y.at[0])
+    send(normg.at[yp * 2 + c], normg.at[yp * 2 + c], sent.at[4], nb_c.at[yp], cdev)
+    at_forward_z(z2, xp, True)
     for q in range(2):
         ff_own_z(q)
-        ff_own_x(q)
-    at_forward_x(z2)
-    arrived(normg.at[yp * 2 + c], nb_y.at[0])
-    send(normg.at[yp * 2 + c], normg.at[yp * 2 + c], sent.at[4], nb_c.at[yp], cdev)
-    at_forward_x(z1)
-    at_forward_x(z3)
     own_cot = cotr.at[pl.ds(head * slots, slots)]
-    send(own_cot, own_cot, sent.at[7], bg_y.at[0], ydev)
-    send(own_cot, own_cot, sent.at[7], bg_c.at[y], cdev)
 
     arrived(normg.at[y * 2 + cp], nb_c.at[y])
     arrived(normg.at[yp * 2 + cp], nb_c.at[yp])
@@ -609,14 +614,18 @@
             media_n[m, rows, :] = norm_rows(media_v[m, rows, :].astype(f32), 0)
         return carry
 
+    local[6].wait()
+    lax.fori_loop(0, slots, norm_latent, 0)
+    at_forward_z(z1, xp, False)
+    at_forward_y(img)
+    at_forward_y(z * n_x + xp)
+    at_forward_z(z3, xp, False)
+    send(own_cot, own_cot, sent.at[7], bg_y.at[0], ydev)
+    send(own_cot, own_cot, sent.at[7], bg_c.at[y], cdev)
     local[7].wait()
-    lax.fori_loop(0, slots, norm_latent, 0)
-    at_forward_y(img)
-    at_forward_y(z2 * n_x + x)
-    local[8].wait()
     blocks = media_v.shape[0]
     step = blocks // 4
-    order = [z * n_x + xp, z1 * n_x + x, z3 * n_x + x, z2 * n_x + xp, z1 * n_x + xp, z3 * n_x + xp]
+    order = [z2 * n_x + x, z1 * n_x + x, z3 * n_x + x, z2 * n_x + xp, z1 * n_x + xp, z3 * n_x + xp]
     for r in range(4):
         lax.fori_loop(r * step, (r + 1) * step, norm_media, 0)
         at_forward_y(order[r])
@@ -643,8 +652,8 @@
     turn_latent(latent_n, latent_t, width)
     at_forward_y(order[4])
     lax.fori_loop(0, blocks * queries // 128, turn_media, 0)
+    at_forward_y(order[5])
     ff_forward(0)
-    at_forward_y(order[5])
 
     for ii in range(8):
         for yy in range(2):
@@ -681,9 +690,8 @@
         kv_media[:, :, tile(t)] = dot_nn(media_rows_n, weight).astype(bf16).reshape(groups, 256, 256)
         return carry
 
-    lax.fori_loop(0, width // 512, kv_step, 0)
+    lax.fori_loop(0, width // 256, kv_step, 0)
     ff_forward(1)
-    lax.fori_loop(width // 512, width // 256, kv_step, 0)
 
     def lane_mask(hh, dtype):
         lane = lax.broadcasted_iota(jnp.int32, (1, 256), 1)
@@ -732,9 +740,8 @@
         send(piece, piece, sent.at[8], hd_c.at[m], cdev)
         return carry
 
-    lax.fori_loop(0, 2, forward_image, 0)
+    lax.fori_loop(0, slots, forward_image, 0)
     ff_forward(2)
-    lax.fori_loop(2, slots, forward_image, 0)
 
     other = yp * 2 + c
     cot_other = cotr.at[pl.ds(other * slots, slots)]
@@ -758,7 +765,6 @@
         lax.fori_loop(0, all_rows // 128, body, 0)
 
     turn_rows(cotr, 1)
-    ff_forward(3)
 
     act_at = 4 * slots
 
@@ -809,7 +815,9 @@
         return lax.fori_loop(0, 2, over_parts, carry)
 
     lax.fori_loop(0, slots, hid_near, 0)
-    lax.fori_loop(0, 3, ff_near, 0)
+    lax.fori_loop(0, 2, ff_near, 0)
+    ff_forward(3)
+    lax.fori_loop(2, 3, ff_near, 0)
     lax.fori_loop(0, slots, hid_forward, 0)
     lax.fori_loop(0, slots, hid_far, 0)
     turn_rows(hid, 0)
@@ -1143,11 +1151,11 @@
     latent_copy.wait()
     arrived(media_v, outs.at[1])
     arrived(normg.at[0, :, 0:384], sent.at[0])
-    arrived(slab.at[0:30], sent.at[1])
+    arrived(slab.at[0:29], sent.at[1])
 
     @pl.when(mid)
     def _():
-        arrived(slab.at[0:2], sent.at[1])
+        arrived(slab.at[0:4], sent.at[1])
         arrived(wide.at[0], sent.at[5])
 
     arrived(normg.at[0, :, 0:512], sent.at[2])
@@ -1166,6 +1174,37 @@
     arrived(gyr_v.at[0:3], sent.at[16])
     arrived(gyr, sent.at[17])
     arrived(gzr.at[0:3], sent.at[18])
+
+
+def finish_kernel(norms, *refs):
+    gains_out, biases_out = refs[8:10]
+    sources, targets, stage = refs[:8], refs[10:18], refs[18:26]
+    sem_in, sem_out = refs[26:28]
+    part = gains_out.shape[1]
+    head = lax.axis_index("head")
+    pieces = []
+    for i in range(8):
+        rows = sources[i].shape[0]
+        count = 4 if rows % 4 == 0 and i == 1 else 1
+        size = rows // count
+        for j in range(count):
+            at = slice(j * size, (j + 1) * size)
+            pieces.append(
+                (
+                    pltpu.make_async_copy(sources[i].at[at], stage[i].at[at], sem_in.at[i, j]),
+                    pltpu.make_async_copy(stage[i].at[at], targets[i].at[at], sem_out.at[i, j]),
+                )
+            )
+    for read, write in pieces:
+        read.start()
+    rolled = pltpu.roll(norms[...], (128 - head * part) % 128, 1)
+    gains_out[...] = rolled[0:3, 0:part]
+    biases_out[...] = rolled[3:6, 0:part]
+    for read, write in pieces:
+        read.wait()
+        write.start()
+    for read, write in pieces:
+        write.wait()
 
 
 def block_plan(
@@ -1187,11 +1226,6 @@
     hidden = up_weight.shape[1]
     rows_up = up_weight.shape[0]
     part = norm_gains.shape[1]
-    head = lax.axis_index("head")
-    norm_rows = jnp.concatenate([norm_gains, norm_biases], axis=0).astype(jnp.float32)
-    norm_tile = lax.dynamic_update_slice(
-        jnp.zeros((8, 128), jnp.float32), norm_rows, (0, head * part)
-    )
     blocks = slots * patches // 64
     bf16, f32 = jnp.bfloat16, jnp.float32
     shape = jax.ShapeDtypeStruct
@@ -1214,7 +1248,7 @@
             shape(up_weight.shape, f32),
             shape(down_weight.shape, f32),
         ),
-        in_specs=[smem] + [hbm] * 7 + [vmem, hbm],
+        in_specs=[smem] + [hbm] * 7 + [vmem] * 3,
         out_specs=(hbm, hbm, hbm, vmem, vmem, vmem, vmem, vmem, vmem),
         scratch_shapes=[
             pltpu.VMEM((32, 64, width), bf16),
@@ -1254,9 +1288,9 @@
             pltpu.VMEM((3, 8, width), f32),
             pltpu.VMEM((4, 8, 128), f32),
             pltpu.VMEM((4, 64, width), bf16),
-            dma((12,)),
-            dma((4,)),
-            dma((4,)),
+            dma((11,)),
+            dma((4, 2)),
+            dma((1,)),
             dma((8,)),
             dma((8, 2)),
             dma((4, 4)),
@@ -1296,22 +1330,27 @@
         output_weight,
         up_weight,
         down_weight,
-        norm_tile,
-    )
-    new, media_grad, latent_grad, norms, query_grad, key_value_grad, output_grad, up_grad, down_grad = outs
-    norms = lax.dynamic_slice(norms, (0, head * part), (6, part))
+        norm_gains,
+        norm_biases,
+    )
+    norms = outs[3]
+    rest = outs[:3] + outs[4:]
+    done = pl.pallas_call(
+        finish_kernel,
+        out_shape=(shape((3, part), f32), shape((3, part), f32)) + tuple(shape(v.shape, v.dtype) for v in rest),
+        in_specs=[vmem] + [hbm] * 8,
+        out_specs=(vmem, vmem) + (hbm,) * 8,
+        scratch_shapes=[pltpu.VMEM(v.shape, v.dtype) for v in rest] + [dma((8, 4)), dma((8, 4))],
+        compiler_params=pltpu.CompilerParams(vmem_limit_bytes=67043328),
+    )(norms, *rest)
+    gains_grad, biases_grad, new, media_grad, latent_grad = done[:5]
     return (
         new.reshape(latent_rows.shape),
         media_grad.reshape(media_patches.shape),
         latent_grad.reshape(latent_rows.shape),
-        norms[0:3],
-        norms[3:6],
-        query_grad,
-        key_value_grad,
-        output_grad,
-        up_grad,
-        down_grad,
-    )
+        gains_grad,
+        biases_grad,
+    ) + tuple(done[5:])
 
 
 def block_fits(mesh):

time: 167 us -> 157 us (0.940)
  local copies, waits for them, and re-layouts: 12.4 us -> 0 us
  Pallas kernels: 152 us -> 156 us
    unnamed x22 -> x0, local copies, waits for them, and re-layouts: 10.7 us -> none
    pallas_call x0 -> x1, Pallas kernels: none -> 6.25 us  [block_plan(): pl.pallas_call(finish_kernel, out_shape=(shape((3, part), f32), shape((3,...]
    pallas_call x1, Pallas kernels: 152 us -> 149 us  [block_plan(): pl.pallas_call(block_kernel, out_shape=(shape((slots, queries, width), bf...]
where the time goes in v4:
time: 157 us
  Pallas kernels  156 us (99%)
    pallas_call x1, Pallas kernels, block_plan(): pl.pallas_call(block_kernel, out_shape=(shape((slots, queries, width), bf...  149 us
    pallas_call x1, Pallas kernels, block_plan(): pl.pallas_call(finish_kernel, out_shape=(shape((3, part), f32), shape((3,...  6.25 us

profile of v4, /device:TPU:0, one launch (start us, length us, event | category | flops | bytes accessed | tf_op | source)
XLA Modules:
  0.0 157.1 jit_solution(769257716805082062)
XLA Ops:
  1.3 149.4 %shard_map.186 = (bf16[5,64,1024]{2,1,0:T(8,128)(2,1)}, bf16[20,64,1024]{2,1,0:T(8,128)(2,1)}, bf16[5,64,1024]{2,1,0:T(8,128)(2,1)}, f32[8,128]{1,0:T(8,128)}, f...) custom-call(s32[1]{0:T(128)S(6)} %copy.21.counts, ...), custom_call_target="tpu_custom_call" | custom-call | tf_op jit(solution)/shard_map/pallas_call | solution.py:1238
  150.7 6.2 %shard_map.187 = (f32[3,32]{1,0:T(4,128)}, f32[3,32]{1,0:T(4,128)}, bf16[5,64,1024]{2,1,0:T(8,128)(2,1)}, bf16[20,64,1024]{2,1,0:T(8,128)(2,1)}, bf16[5,64,1024]...) custom-call(f32[8,128]{1,0:T(8,128)} %get-tuple-element.29.norms, ...), custom_call_target="tpu_custom_call" | custom-call | tf_op jit(solution)/shard_map/pallas_call | solution.py:1338

commit v5 on v4

--- a/solution.py
+++ b/solution.py
@@ -304,9 +304,9 @@
     down_in,
     gain_in,
     bias_in,
-    new_out,
-    media_out,
-    latent_out,
+    delta_v,
+    media_v,
+    latent_v,
     norm_out,
     query_out,
     key_value_out,
@@ -319,9 +319,7 @@
     hid,
     cotr,
     turned,
-    media_v,
     media_n,
-    latent_v,
     latent_n,
     media_t,
     latent_t,
@@ -340,7 +338,6 @@
     hysend,
     hyrecv,
     hown,
-    delta_v,
     attg_v,
     qgrad_v,
     normg,
@@ -377,7 +374,6 @@
     gr_c,
     gr_z,
     sent,
-    outs,
 ):
     n_z, n_x, n_head = 4, 2, 4
     img = lax.axis_index("img")
@@ -550,19 +546,17 @@
         piece = ff_unit(q, img)
         send(piece, piece, sent.at[6], ff_x.at[z, q], xdev)
 
-    def ff_forward(q):
-        for zz in (z2, z1, z3):
-            piece = ff_unit(q, zz * n_x + x)
-            arrived(piece, ff_z.at[zz, q])
-            if zz is z2:
-
-                @pl.when(mid)
-                def _():
-                    send(piece, piece, sent.at[5], ff_z.at[zz, q], zdev(z1))
-
-            send(piece, piece, sent.at[6], ff_x.at[zz, q], xdev)
-        if q + 2 < 4:
-            ff_own_z(q + 2)
+    def ff_forward(e):
+        q, k = e // 3, e % 3
+        zz = (z2 * (2 - k) * (1 - k) + z1 * 2 * k * (2 - k) + z3 * k * (k - 1)) // 2
+        piece = ff_unit(q, zz * n_x + x)
+        arrived(piece, ff_z.at[zz, q])
+
+        @pl.when(jnp.logical_and(mid, k == 0))
+        def _():
+            send(piece, piece, sent.at[5], ff_z.at[zz, q], zdev(z1))
+
+        send(piece, piece, sent.at[6], ff_x.at[zz, q], xdev)
 
     for q in range(4):
         ff_own_x(q)
@@ -650,14 +644,17 @@
                 )
 
     turn_latent(latent_n, latent_t, width)
+    lax.fori_loop(0, blocks * queries // 128, turn_media, 0)
+    ff_forward(0)
     at_forward_y(order[4])
-    lax.fori_loop(0, blocks * queries // 128, turn_media, 0)
+    ff_forward(1)
     at_forward_y(order[5])
-    ff_forward(0)
 
     for ii in range(8):
         for yy in range(2):
             arrived(slab.at[ii * n_head + yy * 2 + cp], at_c.at[ii, yy])
+    ff_forward(2)
+    ff_own_z(2)
 
     query_full[:, 0] = slab[:, 48:64, 0:inner]
     query_full[:, 1] = slab[:, 48:64, inner:width]
@@ -690,8 +687,13 @@
         kv_media[:, :, tile(t)] = dot_nn(media_rows_n, weight).astype(bf16).reshape(groups, 256, 256)
         return carry
 
-    lax.fori_loop(0, width // 256, kv_step, 0)
-    ff_forward(1)
+    def kv_two(i, carry):
+        ff_forward(3 + i)
+        return lax.fori_loop(2 * i, 2 * i + 2, kv_step, carry)
+
+    lax.fori_loop(0, width // 512, kv_two, 0)
+    ff_forward(5)
+    ff_own_z(3)
 
     def lane_mask(hh, dtype):
         lane = lax.broadcasted_iota(jnp.int32, (1, 256), 1)
@@ -738,10 +740,14 @@
         piece = hid.at[head * slots + m]
         send(piece, piece, sent.at[8], hd_y.at[m], ydev)
         send(piece, piece, sent.at[8], hd_c.at[m], cdev)
+
+        @pl.when(jnp.logical_and(m >= 1, m <= 3))
+        def _():
+            ff_forward(5 + m)
+
         return carry
 
     lax.fori_loop(0, slots, forward_image, 0)
-    ff_forward(2)
 
     other = yp * 2 + c
     cot_other = cotr.at[pl.ds(other * slots, slots)]
@@ -814,17 +820,20 @@
 
         return lax.fori_loop(0, 2, over_parts, carry)
 
+    def ff_near_and_forward(q, carry):
+        ff_near(q, 0)
+        ff_forward(9 + q)
+        return carry
+
     lax.fori_loop(0, slots, hid_near, 0)
-    lax.fori_loop(0, 2, ff_near, 0)
-    ff_forward(3)
-    lax.fori_loop(2, 3, ff_near, 0)
+    lax.fori_loop(0, 3, ff_near_and_forward, 0)
     lax.fori_loop(0, slots, hid_forward, 0)
     lax.fori_loop(0, slots, hid_far, 0)
+    lax.fori_loop(0, 3, ff_far, 0)
     turn_rows(hid, 0)
-    ff_far(0, 0)
     grad_tile(0, 0)
     ff_near(3, 0)
-    lax.fori_loop(1, 4, ff_far, 0)
+    ff_far(3, 0)
 
     def wide_rows(part, q, t):
         return wide[q, pl.ds(t * 4, 4), :, part * 256 : (part + 1) * 256].reshape(512, 256)
@@ -1048,8 +1057,6 @@
             rows = slice(r * half, (r + 1) * half)
             branch = hown[1, m, rows, :] + hyrecv[1, m, rows, :].astype(f32)
             new_v[m, rows, :] = ((mid_v[m, rows, :] + branch) * keep).astype(bf16)
-    new_copy = pltpu.make_async_copy(new_v, new_out, outs.at[0])
-    new_copy.start()
     stage_y(chunk[3])
 
     def media_back(m, carry):
@@ -1062,7 +1069,6 @@
             return carry2
 
         lax.fori_loop(0, 4, over_rows, 0)
-        pltpu.make_async_copy(media_v.at[pl.ds(m * 4, 4)], media_out.at[pl.ds(m * 4, 4)], outs.at[1]).start()
         return carry
 
     def latent_back_tiles(t, carry):
@@ -1081,19 +1087,13 @@
 
     lax.fori_loop(0, width // 512, latent_back_tiles, 0)
     lax.fori_loop(0, slots, latent_back, 0)
-    latent_copy = pltpu.make_async_copy(latent_v, latent_out, outs.at[2])
-    latent_copy.start()
     lax.fori_loop(0, 2, media_back, 0)
     sum_tile(7)
     stage_x(chunk[0])
+    lax.fori_loop(2, 4, media_back, 0)
     stage_x(chunk[1])
-    lax.fori_loop(2, 4, media_back, 0)
-    stage_x(chunk[2])
     stage_z(chunk[0], False)
-    stage_z(chunk[1], False)
     lax.fori_loop(4, 5, media_back, 0)
-    stage_x(chunk[3])
-    stage_z(chunk[2], False)
 
     for j in range(6):
         gsend[0, j : j + 1, :] = jnp.sum(gacc[j], axis=0, keepdims=True)
@@ -1101,21 +1101,21 @@
     send(gsend.at[0], gyr.at[0], sent.at[17], gr_c.at[0], cdev)
     arrived(gyr.at[0], gr_c.at[0])
     gsend[1] = gsend[0] + gyr[0]
-    send(gsend.at[1], gyr.at[1], sent.at[17], gr_c.at[1], ydev)
+    send(gsend.at[1], gyr.at[1], sent.at[17], gr_c.at[1], xdev)
+    stage_z(chunk[1], False)
     arrived(gyr.at[1], gr_c.at[1])
     gsend[2] = gsend[1] + gyr[1]
-    send(gsend.at[2], gyr.at[2], sent.at[17], gr_c.at[2], xdev)
-    arrived(gyr.at[2], gr_c.at[2])
-    gsend[3] = gsend[2] + gyr[2]
     for k in near:
         zz = zat(k)
-        send(gsend.at[3, :, lanes(zz * n_x + x)], gzr.at[z], sent.at[18], gr_z.at[z], zdev(zz))
-    total = gsend[3, :, lanes(img)]
+        send(gsend.at[2, :, lanes(zz * n_x + x)], gzr.at[z], sent.at[18], gr_z.at[z], zdev(zz))
+    stage_x(chunk[2])
+    total = gsend[2, :, lanes(img)]
     for k in near:
         zz = zat(k)
         arrived(gzr.at[zz], gr_z.at[zz])
         total = total + gzr[zz]
-    norm_out[...] = total
+    gsend[3, :, 0:128] = total
+    send(gsend.at[3, :, 0:128], gyr.at[2, :, 0:128], sent.at[17], gr_c.at[2], ydev)
 
     for part in range(2):
         for k in range(3):
@@ -1137,6 +1137,10 @@
 
     lax.fori_loop(0, hidden // 256, last_sums, 0)
 
+    stage_x(chunk[3])
+    stage_z(chunk[2], False)
+    arrived(gyr.at[2, :, 0:128], gr_c.at[2])
+    norm_out[...] = gsend[3, :, 0:128] + gyr[2, :, 0:128]
     final = stage_z(chunk[3], True)
     for k in near:
         zz = zat(k)
@@ -1147,9 +1151,6 @@
     query_out[0:16, :] = final[48:64, 0:inner]
     query_out[16:32, :] = final[48:64, inner:width]
 
-    new_copy.wait()
-    latent_copy.wait()
-    arrived(media_v, outs.at[1])
     arrived(normg.at[0, :, 0:384], sent.at[0])
     arrived(slab.at[0:29], sent.at[1])
 
@@ -1172,39 +1173,23 @@
     arrived(gyr_v.at[0:8], sent.at[14])
     arrived(gyr_v.at[0:4], sent.at[15])
     arrived(gyr_v.at[0:3], sent.at[16])
-    arrived(gyr, sent.at[17])
+    arrived(gyr.at[0:2], sent.at[17])
+    arrived(gyr.at[2, :, 0:128], sent.at[17])
     arrived(gzr.at[0:3], sent.at[18])
 
 
 def finish_kernel(norms, *refs):
-    gains_out, biases_out = refs[8:10]
-    sources, targets, stage = refs[:8], refs[10:18], refs[18:26]
-    sem_in, sem_out = refs[26:28]
+    sources, gains_out, biases_out, targets, sems = refs[:8], refs[8], refs[9], refs[10:18], refs[18]
+    copies = [pltpu.make_async_copy(sources[i], targets[i], sems.at[i]) for i in range(8)]
+    for copy in copies:
+        copy.start()
     part = gains_out.shape[1]
     head = lax.axis_index("head")
-    pieces = []
-    for i in range(8):
-        rows = sources[i].shape[0]
-        count = 4 if rows % 4 == 0 and i == 1 else 1
-        size = rows // count
-        for j in range(count):
-            at = slice(j * size, (j + 1) * size)
-            pieces.append(
-                (
-                    pltpu.make_async_copy(sources[i].at[at], stage[i].at[at], sem_in.at[i, j]),
-                    pltpu.make_async_copy(stage[i].at[at], targets[i].at[at], sem_out.at[i, j]),
-                )
-            )
-    for read, write in pieces:
-        read.start()
     rolled = pltpu.roll(norms[...], (128 - head * part) % 128, 1)
     gains_out[...] = rolled[0:3, 0:part]
     biases_out[...] = rolled[3:6, 0:part]
-    for read, write in pieces:
-        read.wait()
-        write.start()
-    for read, write in pieces:
-        write.wait()
+    for copy in copies:
+        copy.wait()
 
 
 def block_plan(
@@ -1238,18 +1223,18 @@
     outs = pl.pallas_call(
         block_kernel,
         out_shape=(
-            shape((slots, queries, width), bf16),
-            shape((blocks, 64, width), bf16),
-            shape((slots, queries, width), bf16),
-            shape((8, 128), f32),
-            shape(query_weight.shape, f32),
-            shape(key_value_weight.shape, f32),
-            shape(output_weight.shape, f32),
-            shape(up_weight.shape, f32),
-            shape(down_weight.shape, f32),
+            pltpu.VMEM((slots, queries, width), bf16),
+            pltpu.VMEM((blocks, 64, width), bf16),
+            pltpu.VMEM((slots, queries, width), bf16),
+            pltpu.VMEM((8, 128), f32),
+            pltpu.VMEM(query_weight.shape, f32),
+            pltpu.VMEM(key_value_weight.shape, f32),
+            pltpu.VMEM(output_weight.shape, f32),
+            pltpu.VMEM(up_weight.shape, f32),
+            pltpu.VMEM(down_weight.shape, f32),
         ),
         in_specs=[smem] + [hbm] * 7 + [vmem] * 3,
-        out_specs=(hbm, hbm, hbm, vmem, vmem, vmem, vmem, vmem, vmem),
+        out_specs=(vmem,) * 9,
         scratch_shapes=[
             pltpu.VMEM((32, 64, width), bf16),
             pltpu.VMEM((32, 2, 16, inner), bf16),
@@ -1258,8 +1243,6 @@
             pltpu.VMEM((4 * slots, queries, width), bf16),
             pltpu.VMEM((2, width, all_rows), bf16),
             pltpu.VMEM((blocks, 64, width), bf16),
-            pltpu.VMEM((blocks, 64, width), bf16),
-            pltpu.VMEM((slots, queries, width), bf16),
             pltpu.VMEM((slots, queries, width), bf16),
             pltpu.VMEM((width, slots * patches), bf16),
             pltpu.VMEM((width, rows_latent), bf16),
@@ -1278,7 +1261,6 @@
             pltpu.VMEM((2, slots, queries, width), bf16),
             pltpu.VMEM((2, slots, queries, width), bf16),
             pltpu.VMEM((2, slots, queries, width), f32),
-            pltpu.VMEM((slots, queries, width), bf16),
             pltpu.VMEM((slots, queries, inner), bf16),
             pltpu.VMEM((slots, queries, inner), bf16),
             pltpu.VMEM((4, 8, width), f32),
@@ -1315,10 +1297,9 @@
             dma((3,)),
             dma((4,)),
             dma((19,)),
-            dma((3,)),
         ],
         compiler_params=pltpu.CompilerParams(
-            collective_id=0, has_side_effects=True, vmem_limit_bytes=67043328
+            collective_id=0, has_side_effects=True, vmem_limit_bytes=61796352
         ),
     )(
         media_counts,
@@ -1338,10 +1319,10 @@
     done = pl.pallas_call(
         finish_kernel,
         out_shape=(shape((3, part), f32), shape((3, part), f32)) + tuple(shape(v.shape, v.dtype) for v in rest),
-        in_specs=[vmem] + [hbm] * 8,
+        in_specs=[vmem] * 9,
         out_specs=(vmem, vmem) + (hbm,) * 8,
-        scratch_shapes=[pltpu.VMEM(v.shape, v.dtype) for v in rest] + [dma((8, 4)), dma((8, 4))],
-        compiler_params=pltpu.CompilerParams(vmem_limit_bytes=67043328),
+        scratch_shapes=[dma((8,))],
+        compiler_params=pltpu.CompilerParams(vmem_limit_bytes=4194304),
     )(norms, *rest)
     gains_grad, biases_grad, new, media_grad, latent_grad = done[:5]
     return (

time: 157 us -> 152 us (0.968)
  Pallas kernels: 156 us -> 151 us
    pallas_call x1, Pallas kernels: 6.25 us -> 2.99 us  [block_plan(): pl.pallas_call(finish_kernel, out_shape=(shape((3, part), f32), shape((3,...]
    pallas_call x1, Pallas kernels: 149 us -> 148 us  [block_plan(): pl.pallas_call(block_kernel, out_shape=(pltpu.VMEM((slots, queries, width...]
where the time goes in v5:
time: 152 us
  Pallas kernels  151 us (99%)
    pallas_call x1, Pallas kernels, block_plan(): pl.pallas_call(block_kernel, out_shape=(pltpu.VMEM((slots, queries, width...  148 us

profile of v5, /device:TPU:0, one launch (start us, length us, event | category | flops | bytes accessed | tf_op | source)
XLA Modules:
  0.0 152.1 jit_solution(3790663734058704456)
XLA Ops:
  1.3 147.6 %shard_map.186 = (bf16[5,64,1024]{2,1,0:T(8,128)(2,1)S(1)}, bf16[20,64,1024]{2,1,0:T(8,128)(2,1)S(1)}, bf16[5,64,1024]{2,1,0:T(8,128)(2,1)S(1)}, f32[8,128]{1,0:...) custom-call(s32[1]{0:T(128)S(6)} %copy.21.counts, ...), custom_call_target="tpu_custom_call" | custom-call | tf_op jit(solution)/shard_map/pallas_call | solution.py:1223
  148.9 3.0 %shard_map.187 = (f32[3,32]{1,0:T(4,128)}, f32[3,32]{1,0:T(4,128)}, bf16[5,64,1024]{2,1,0:T(8,128)(2,1)}, bf16[20,64,1024]{2,1,0:T(8,128)(2,1)}, bf16[5,64,1024]...) custom-call(f32[8,128]{1,0:T(8,128)S(1)} %get-tuple-element.29.norms, ...), custom_call_target="tpu_custom_call" | custom-call | tf_op jit(solution)/shard_map/pallas_call | solution.py:1319

commit v6 on v5

--- a/solution.py
+++ b/solution.py
@@ -866,11 +866,11 @@
 
         def to_y(t, carry):
             value = back_rows(left_y, part, t).reshape(slots, queries, 512)
-            hysend[part, :, :, broad(t)] = (value + hrecv[part, 0, :, :, broad(t)].astype(f32)).astype(bf16)
+            hysend[part, t] = (value + hrecv[part, 0, :, :, broad(t)].astype(f32)).astype(bf16)
+            send(hysend.at[part, t], hyrecv.at[part, t], sent.at[10], hp_y.at[part], ydev)
             return carry
 
         lax.fori_loop(0, width // 512, to_y, 0)
-        send(hysend.at[part], hyrecv.at[part], sent.at[10], hp_y.at[part], ydev)
         left_own = rows_of(head)
         arrived(hrecv.at[part, 1], hp_c.at[part, 1])
 
@@ -893,12 +893,12 @@
             ).astype(bf16)
             send(grads.at[q, part, x, zz], zrecv.at[k, part, q], sent.at[12], rf_z.at[k, part], zdev(zz))
 
-    lax.fori_loop(1, 4, grad_tile, 0)
+    grad_tile(1, 0)
     sum_tile(0)
-    sum_tile(1)
     arrived(hsend, sent.at[9])
     head_sum(1)
-    sum_tile(2)
+    lax.fori_loop(2, 4, grad_tile, 0)
+    sum_tile(1)
 
     gacc[...] = jnp.zeros_like(gacc)
 
@@ -914,11 +914,11 @@
             g - jnp.mean(g, axis=-1, keepdims=True) - xhat * jnp.mean(g * xhat, axis=-1, keepdims=True)
         )
 
-    sum_tile(3)
+    sum_tile(2)
     arrived(hyrecv.at[0], hp_y.at[0])
 
     def mid_back(m, carry):
-        upper = hown[0, m] + hyrecv[0, m].astype(f32)
+        upper = hown[0, m] + jnp.concatenate([hyrecv[0, 0, m], hyrecv[0, 1, m]], axis=-1).astype(f32)
         back = norm_back(mid_v[m], 2, upper)
         total = cotr[head * slots + m].astype(f32) + back
         hown[0, m] = total
@@ -947,7 +947,7 @@
         return carry
 
     lax.fori_loop(0, width // 512, out_grad_step, 0)
-    sum_tile(4)
+    sum_tile(3)
 
     def back_pair(m, g):
         q_rows, k_media, k_latent, p_media, p_latent = probabilities(m, g)
@@ -974,7 +974,7 @@
 
     lax.fori_loop(0, slots, back_image, 0)
 
-    sum_tile(5)
+    sum_tile(4)
 
     gcr = hid
     gyr_v = media_n
@@ -1008,7 +1008,7 @@
             )
 
     def stage_y(zz):
-        for xx in range(2):
+        for xx in (xp, x):
             ii = zz * n_x + xx
             arrived(gcr.at[pl.ds(ii * 2, 2)], ra_c.at[ii])
             uu = gunit(ii, yp, c)
@@ -1046,7 +1046,7 @@
     stage_y(chunk[1])
     kv_grad_chunk(chunk[3])
     stage_y(chunk[2])
-    sum_tile(6)
+    sum_tile(5)
 
     arrived(hyrecv.at[1], hp_y.at[1])
     new_v = delta_v
@@ -1055,7 +1055,9 @@
         keep = jnp.clip(filled - m, 0, 1).astype(f32)
         for r in range(2):
             rows = slice(r * half, (r + 1) * half)
-            branch = hown[1, m, rows, :] + hyrecv[1, m, rows, :].astype(f32)
+            branch = hown[1, m, rows, :] + jnp.concatenate(
+                [hyrecv[1, 0, m, rows, :], hyrecv[1, 1, m, rows, :]], axis=-1
+            ).astype(f32)
             new_v[m, rows, :] = ((mid_v[m, rows, :] + branch) * keep).astype(bf16)
     stage_y(chunk[3])
 
@@ -1087,6 +1089,7 @@
 
     lax.fori_loop(0, width // 512, latent_back_tiles, 0)
     lax.fori_loop(0, slots, latent_back, 0)
+    sum_tile(6)
     lax.fori_loop(0, 2, media_back, 0)
     sum_tile(7)
     stage_x(chunk[0])
@@ -1258,8 +1261,8 @@
             pltpu.VMEM((3, 2, 4, rows_up, 256), bf16),
             pltpu.VMEM((2, slots, queries, width), bf16),
             pltpu.VMEM((2, 2, slots, queries, width), bf16),
-            pltpu.VMEM((2, slots, queries, width), bf16),
-            pltpu.VMEM((2, slots, queries, width), bf16),
+            pltpu.VMEM((2, 2, slots, queries, width // 2), bf16),
+            pltpu.VMEM((2, 2, slots, queries, width // 2), bf16),
             pltpu.VMEM((2, slots, queries, width), f32),
             pltpu.VMEM((slots, queries, inner), bf16),
             pltpu.VMEM((slots, queries, inner), bf16),

time: 152 us -> 151 us (level)
  Pallas kernels: 151 us -> 149 us
    pallas_call x1, Pallas kernels: 148 us -> 146 us  [block_plan(): pl.pallas_call(block_kernel, out_shape=(pltpu.VMEM((slots, queries, width...]
where the time goes in v6:
time: 151 us; the launch traced here: 150 us
  Pallas kernels  149 us (99%)
    pallas_call x1, Pallas kernels, block_plan(): pl.pallas_call(block_kernel, out_shape=(pltpu.VMEM((slots, queries, width...  146 us

profile of v6, /device:TPU:0, one launch (start us, length us, event | category | flops | bytes accessed | tf_op | source)
XLA Modules:
  0.0 150.4 jit_solution(12481732369559378543)
XLA Ops:
  1.3 145.9 %shard_map.186 = (bf16[5,64,1024]{2,1,0:T(8,128)(2,1)S(1)}, bf16[20,64,1024]{2,1,0:T(8,128)(2,1)S(1)}, bf16[5,64,1024]{2,1,0:T(8,128)(2,1)S(1)}, f32[8,128]{1,0:...) custom-call(s32[1]{0:T(128)S(6)} %copy.21.counts, ...), custom_call_target="tpu_custom_call" | custom-call | tf_op jit(solution)/shard_map/pallas_call | solution.py:1226
  147.2 3.0 %shard_map.187 = (f32[3,32]{1,0:T(4,128)}, f32[3,32]{1,0:T(4,128)}, bf16[5,64,1024]{2,1,0:T(8,128)(2,1)}, bf16[20,64,1024]{2,1,0:T(8,128)(2,1)}, bf16[5,64,1024]...) custom-call(f32[8,128]{1,0:T(8,128)S(1)} %get-tuple-element.29.norms, ...), custom_call_target="tpu_custom_call" | custom-call | tf_op jit(solution)/shard_map/pallas_call | solution.py:1322

commit v7 on v6

--- a/solution.py
+++ b/solution.py
@@ -894,10 +894,10 @@
             send(grads.at[q, part, x, zz], zrecv.at[k, part, q], sent.at[12], rf_z.at[k, part], zdev(zz))
 
     grad_tile(1, 0)
-    sum_tile(0)
     arrived(hsend, sent.at[9])
     head_sum(1)
     lax.fori_loop(2, 4, grad_tile, 0)
+    sum_tile(0)
     sum_tile(1)
 
     gacc[...] = jnp.zeros_like(gacc)

time: 151 us -> 156 us (1.033)
  Pallas kernels: 149 us -> 154 us
    pallas_call x1, Pallas kernels: 146 us -> 151 us  [block_plan(): pl.pallas_call(block_kernel, out_shape=(pltpu.VMEM((slots, queries, width...]
where the time goes in v7:
time: 156 us
  Pallas kernels  154 us (99%)
    pallas_call x1, Pallas kernels, block_plan(): pl.pallas_call(block_kernel, out_shape=(pltpu.VMEM((slots, queries, width...  151 us

profile of v7, /device:TPU:0, one launch (start us, length us, event | category | flops | bytes accessed | tf_op | source)
XLA Modules:
  0.0 155.8 jit_solution(9352594298717329604)
XLA Ops:
  1.3 151.3 %shard_map.186 = (bf16[5,64,1024]{2,1,0:T(8,128)(2,1)S(1)}, bf16[20,64,1024]{2,1,0:T(8,128)(2,1)S(1)}, bf16[5,64,1024]{2,1,0:T(8,128)(2,1)S(1)}, f32[8,128]{1,0:...) custom-call(s32[1]{0:T(128)S(6)} %copy.21.counts, ...), custom_call_target="tpu_custom_call" | custom-call | tf_op jit(solution)/shard_map/pallas_call | solution.py:1226
  152.6 3.0 %shard_map.187 = (f32[3,32]{1,0:T(4,128)}, f32[3,32]{1,0:T(4,128)}, bf16[5,64,1024]{2,1,0:T(8,128)(2,1)}, bf16[20,64,1024]{2,1,0:T(8,128)(2,1)}, bf16[5,64,1024]...) custom-call(f32[8,128]{1,0:T(8,128)S(1)} %get-tuple-element.29.norms, ...), custom_call_target="tpu_custom_call" | custom-call | tf_op jit(solution)/shard_map/pallas_call | solution.py:1322
